TPU v7x, 32 devices: a whole 2x2x4 slice. The times are simulated.
32 devices in a mesh: loop: 16 (over z, y, core), narrow: 2 (over x).
Axes of the slice: x: 2, y: 2, z: 4, core: 2. Of those that a mesh axis runs over, the one named last changes fastest.
Arguments:
- queries: bfloat16 [8192, 4096], P(('loop', 'narrow')), may hold values from -2 to 2
- passages: bfloat16 [64, 4096], P('loop'), may hold values from -10 to 10
- pos_ids: int32 [8192], P(('loop', 'narrow')), may hold values from 0 to 63
- neg_ids: int32 [8192, 32], P(('loop', 'narrow')), may hold values from 0 to 63
- neg_mask: int32 [8192, 32], P(('loop', 'narrow')), may hold values 0 or 1
- neg_counts: int32 [8192], P(('loop', 'narrow')), may hold values from 0 to 32
- d_loss: float32 [8192], P(('loop', 'narrow')), may hold values from -6 to 6
Outputs:
- query_loss: float32 [8192], P(('loop', 'narrow'))
- grad_queries: bfloat16 [8192, 4096], P(('loop', 'narrow'))
- grad_passages: bfloat16 [64, 4096], P('loop')
Inputs may be any that keep to these rules, and one draw needn't show every extreme that they name: `neg_counts`: slots at or beyond a query's count are padding.
All inputs are finite; a program needn't handle non-finite values. No bound on the sum of `neg_mask` on one device may be relied on, other than what follows from the above.
Results may differ from a plain program's by a relative error of at most 0.0058.
Values may be sent and summed in bfloat16 or wider, within the bound.
No kernel may reach another device: no remote copies, remote signals or barrier semaphores. Data moves between devices by JAX's collectives and lax.ppermute only.
A program may use at most 64 MiB of HBM per device.

v0:
```python
import functools

import jax
import jax.numpy as jnp
from jax import lax
from jax.experimental import pallas as pl
from jax.experimental.pallas import tpu as pltpu
from jax.sharding import PartitionSpec as P


logit_scale = 50.0
norm_eps = 1e-06


VMEM = pl.BlockSpec(memory_space=pltpu.VMEM)
SMEM = pl.BlockSpec(memory_space=pltpu.SMEM)
ROWS = (((1,), (1,)), ((), ()))


def stage_masks(size):
    bits = [1 << b for b in range(size.bit_length() - 1)][::-1]
    first = [0, bits[1] | 1, bits[0] | 1, bits[0] | bits[1] | 1]
    return [first] + [[0, b | 1] for b in bits[2:]]


def swap(x, axis, size, mask):
    return lax.ppermute(x, axis, [(i, i ^ mask) for i in range(size)])


def wide(x):
    return x.astype(jnp.float32)


LIMIT = pltpu.CompilerParams(vmem_limit_bytes=16 * 1024 * 1024)
WIDE_LIMIT = pltpu.CompilerParams(vmem_limit_bytes=60 * 1024 * 1024)


def cost(flops, moved):
    return pl.CostEstimate(flops=flops, bytes_accessed=moved, transcendentals=0)


def passage_ids(stages, block, shape, me):
    row = lax.broadcasted_iota(jnp.int32, shape, 0)
    place = row // block
    digits, owner = place, jnp.full(shape, me, jnp.int32)
    for masks in stages:
        digit = digits % len(masks)
        digits = digits // len(masks)
        chosen = jnp.zeros(shape, jnp.int32)
        for k, m in enumerate(masks[1:]):
            chosen = jnp.where(digit == k + 1, m, chosen)
        owner = owner ^ chosen
    return owner * block + (row - place * block)


def prepare_kernel(
    stages, block, me_ref, ids_hbm, mask_hbm, count_hbm, q_hbm, w_ref, qs_ref, q_ref, ids_ref, mask_ref, count_ref, sems
):
    parts = sems.shape[0] - 3
    rows = q_ref.shape[0] // parts
    small = [
        pltpu.make_async_copy(src, dst, sems.at[parts + k])
        for k, (src, dst) in enumerate(((ids_hbm, ids_ref), (mask_hbm, mask_ref), (count_hbm, count_ref)))
    ]
    large = [
        pltpu.make_async_copy(q_hbm.at[pl.ds(k * rows, rows)], q_ref.at[pl.ds(k * rows, rows)], sems.at[k])
        for k in range(parts)
    ]
    for copy in small + large:
        copy.start()
    columns = passage_ids(stages, block, w_ref.shape, me_ref[0])
    for copy in small:
        copy.wait()
    slots = ids_ref.shape[0]
    slot = lax.broadcasted_iota(jnp.int32, ids_ref.shape, 0)
    named = jnp.where((mask_ref[...] == 1) & (slot < count_ref[...]), ids_ref[...], -1)
    weights = jnp.ones(w_ref.shape, jnp.float32)
    for k in range(slots):
        weights = weights + jnp.where(named[k : k + 1] == columns, 1.0, 0.0)
    w_ref[...] = weights
    scales = []
    for k in range(parts):
        large[k].wait()
        f = wide(q_ref[k * rows : (k + 1) * rows])
        scales.append(lax.rsqrt(jnp.sum(f * f, axis=1, keepdims=True) + norm_eps))
    scale = jnp.concatenate(scales, axis=0)
    qs_ref[...] = jnp.broadcast_to(scale, (scale.shape[0], 128)).T[:1]


def raw_and_scale(refs, q):
    rows = jnp.concatenate([r[...] for r in refs], axis=0)
    f = wide(rows)
    scale = lax.rsqrt(jnp.sum(f * f, axis=1, keepdims=True) + norm_eps)
    return lax.dot_general(rows, q, ROWS, preferred_element_type=jnp.float32), scale


def first_kernel(n, *refs):
    q_ref, raw_ref, scale_ref = refs[n:]
    raw, scale = raw_and_scale(refs[:n], q_ref[...])
    raw_ref[...] = raw
    scale_ref[...] = jnp.broadcast_to(scale, scale_ref.shape)


def loss_kernel(n, stages, block, *refs):
    me_ref, q_ref, rawa_ref, scalea_ref, w_ref, qs_ref, pos_ref, dl_ref = refs[n : n + 8]
    sent_ref, pa_ref, qc_ref, loss_ref, inner_ref = refs[n + 8 :]
    half = rawa_ref.shape[0]
    q = q_ref[...]
    qs = qs_ref[...]
    rawb, scaleb = raw_and_scale(refs[:n], q)
    raw = jnp.concatenate([rawa_ref[...], rawb], axis=0)
    scale = jnp.concatenate([scalea_ref[:, :1], scaleb], axis=0)
    scores = logit_scale * (raw * scale * qs)
    terms = w_ref[...] * jnp.exp(scores)
    denom = jnp.sum(terms, axis=0, keepdims=True)
    chosen = passage_ids(stages, block, scores.shape, me_ref[0]) == pos_ref[...]
    coef = (logit_scale * dl_ref[...]) * (terms / denom - jnp.where(chosen, 1.0, 0.0))
    pcoef = (coef * qs).astype(jnp.bfloat16)
    sent_ref[...] = jnp.dot(pcoef[half:], q, preferred_element_type=jnp.float32).astype(jnp.bfloat16)
    pa_ref[...] = pcoef[:half]
    qcoef = (coef * qs * scale).astype(jnp.bfloat16)
    qc_ref[...] = qcoef
    loss_ref[...] = jnp.log(denom) - jnp.sum(jnp.where(chosen, scores, 0.0), axis=0, keepdims=True)
    inner_ref[...] = jnp.sum(wide(qcoef) * raw, axis=0, keepdims=True) * qs * qs


def kept_kernel(pa_ref, q_ref, kept_ref):
    kept_ref[...] = jnp.dot(pa_ref[...], q_ref[...], preferred_element_type=jnp.float32)


def query_kernel(n, *refs):
    qc_ref, q_ref, inner_ref, out_ref = refs[n:]
    step = out_ref.shape[1]
    at = pl.ds(pl.multiple_of(pl.program_id(0) * step, step), step)
    rows = jnp.concatenate([r[:, at] for r in refs[:n]], axis=0)
    qdir = lax.dot_general(qc_ref[...], rows, (((0,), (0,)), ((), ())), preferred_element_type=jnp.float32)
    inner = jnp.broadcast_to(inner_ref[...], (128, inner_ref.shape[1])).T[:, :1]
    out_ref[...] = (qdir - wide(q_ref[:, at]) * inner).astype(jnp.bfloat16)


def passage_kernel(n, p_ref, total_ref, *refs):
    out_ref = refs[n]
    pdir = total_ref[...]
    for r in refs[:n]:
        pdir = pdir + wide(r[...])
    f = wide(p_ref[...])
    scale = lax.rsqrt(jnp.sum(f * f, axis=1, keepdims=True) + norm_eps)
    unit = f * scale
    inner = jnp.sum(unit * pdir, axis=1, keepdims=True)
    out_ref[...] = (scale * (pdir - unit * inner)).astype(jnp.bfloat16)


def make_local(loop, narrow):
    stages = stage_masks(loop)

    def local(queries, passages, pos_ids, neg_ids, neg_mask, neg_counts, d_loss):
        return body(queries, passages, pos_ids, neg_ids, neg_mask, neg_counts, d_loss)

    def body(queries, passages, pos_ids, neg_ids, neg_mask, neg_counts, d_loss):
        me = lax.axis_index("loop")
        me_arr = me.astype(jnp.int32).reshape(1)
        block, width = passages.shape
        count = queries.shape[0]
        pool_size = loop * block

        first = [passages] + [swap(passages, "loop", loop, m) for m in stages[0][1:]]
        pool = [jnp.concatenate(first[k : k + 2], axis=0) for k in (0, 2)]
        for at, (_, m) in enumerate(stages[1:]):
            moved = [swap(t, "loop", loop, m) for t in pool]
            pool = pool + moved
            if at < len(stages) - 3:
                pool = [jnp.concatenate(pool, axis=0)]
        n = len(pool) // 2
        half = pool_size // 2

        f32 = jnp.float32
        parts = 4
        weights, qs = pl.pallas_call(
            functools.partial(prepare_kernel, stages, block),
            out_shape=(
                jax.ShapeDtypeStruct((pool_size, count), f32),
                jax.ShapeDtypeStruct((1, count), f32),
            ),
            in_specs=[SMEM] + [pl.BlockSpec(memory_space=pltpu.HBM)] * 4,
            out_specs=(VMEM,) * 2,
            scratch_shapes=[
                pltpu.VMEM(queries.shape, queries.dtype),
                pltpu.VMEM(neg_ids.shape[::-1], jnp.int32),
                pltpu.VMEM(neg_ids.shape[::-1], jnp.int32),
                pltpu.VMEM((1, count), jnp.int32),
                pltpu.SemaphoreType.DMA((parts + 3,)),
            ],
            cost_estimate=cost(10000000, 3000000),
            compiler_params=WIDE_LIMIT,
            name="prepare",
        )(me_arr, neg_ids.T, neg_mask.T, neg_counts.reshape(1, count), queries)
        rawa, scalea = pl.pallas_call(
            functools.partial(first_kernel, n),
            out_shape=(jax.ShapeDtypeStruct((half, count), f32), jax.ShapeDtypeStruct((half, 128), f32)),
            in_specs=[VMEM] * (n + 1),
            out_specs=(VMEM, VMEM),
            cost_estimate=cost(2 * half * count * width, 2000000),
            compiler_params=LIMIT,
            name="first_scores",
        )(*pool[:n], queries)
        sent, pa, qc, loss, inner = pl.pallas_call(
            functools.partial(loss_kernel, n, stages, block),
            out_shape=(
                jax.ShapeDtypeStruct((half, width), jnp.bfloat16),
                jax.ShapeDtypeStruct((half, count), jnp.bfloat16),
                jax.ShapeDtypeStruct((pool_size, count), jnp.bfloat16),
                jax.ShapeDtypeStruct((1, count), f32),
                jax.ShapeDtypeStruct((1, count), f32),
            ),
            in_specs=[VMEM] * n + [SMEM] + [VMEM] * 7,
            out_specs=(VMEM,) * 5,
            cost_estimate=cost(4 * half * count * width, 2000000),
            compiler_params=LIMIT,
            name="loss",
        )(*pool[n:], me_arr, queries, rawa, scalea, weights, qs, pos_ids.reshape(1, count), d_loss.reshape(1, count))
        total = pl.pallas_call(
            kept_kernel,
            out_shape=jax.ShapeDtypeStruct((half, width), f32),
            in_specs=[VMEM] * 2,
            out_specs=VMEM,
            cost_estimate=cost(2 * half * count * width, 2000000),
            compiler_params=LIMIT,
            name="kept_terms",
        )(pa, queries)

        total = total + wide(swap(sent, "loop", loop, stages[-1][1]))
        for masks in stages[:-1][::-1]:
            part = total.shape[0] // len(masks)
            moved = [
                swap(total[k * part : (k + 1) * part].astype(jnp.bfloat16), "loop", loop, masks[k])
                for k in range(len(masks) - 1, 0, -1)
            ]
            total = total[:part]
            for t in moved:
                total = total + wide(t)
        moved = []
        for b in range(narrow.bit_length() - 1):
            if moved:
                total = total + wide(moved.pop())
            moved.append(swap(total.astype(jnp.bfloat16), "narrow", narrow, 1 << b))

        step = 512
        grad_queries = pl.pallas_call(
            functools.partial(query_kernel, 2 * n),
            out_shape=jax.ShapeDtypeStruct(queries.shape, jnp.bfloat16),
            grid=(width // step,),
            in_specs=[VMEM] * (2 * n + 3),
            out_specs=pl.BlockSpec((count, step), lambda i: (0, i)),
            cost_estimate=cost(2 * pool_size * count * width, 5000000),
            compiler_params=LIMIT,
            name="query_gradients",
        )(*pool, qc, queries, inner)
        grad_passages = pl.pallas_call(
            functools.partial(passage_kernel, len(moved)),
            out_shape=jax.ShapeDtypeStruct(passages.shape, jnp.bfloat16),
            in_specs=[VMEM] * (2 + len(moved)),
            out_specs=VMEM,
            cost_estimate=cost(1000000, 200000),
            compiler_params=LIMIT,
            name="passage_gradients",
        )(passages, total, *moved)
        return loss.reshape(count), grad_queries, grad_passages

    return local


def solution(mesh):
    return jax.shard_map(
        make_local(mesh.shape["loop"], mesh.shape["narrow"]),
        mesh=mesh,
        in_specs=(
            P(("loop", "narrow"), None),
            P("loop", None),
            P(("loop", "narrow")),
            P(("loop", "narrow"), None),
            P(("loop", "narrow"), None),
            P(("loop", "narrow")),
            P(("loop", "narrow")),
        ),
        out_specs=(P(("loop", "narrow")), P(("loop", "narrow"), None), P("loop", None)),
        check_vma=False,
    )
```

profile of v0, /device:TPU:0, one launch (start us, length us, event | category | flops | bytes accessed | tf_op | source)
XLA Modules:
  0.0 42.2 jit_solution(2263519645337829346)
XLA Ops:
  0.6 0.0 copy-start
  0.6 3.6 %collective-permute-start.2 = (bf16[4,4096]{1,0:T(4,128)(2,1)}, bf16[4,4096]{1,0:T(4,128)(2,1)S(1)}, u32[]{:S(2)}, u32[]{:S(2)}) collective-permute-start(bf16[4,4096]{1,0:T(4,128)(2,1)} %p_ref.1), channel_id=1, source_target_pairs={{0,18},{2,16},{4,22},{6,20},{8,26},{10,24},{12,30},{14,28},{16,2},... | collective-permute-start | bytes 98312 | tf_op jit(solution)/shard_map/ppermute | solution.py:27
  4.2 1.6 %collective-permute-start.3 = (bf16[4,4096]{1,0:T(4,128)(2,1)}, bf16[4,4096]{1,0:T(4,128)(2,1)S(1)}, u32[]{:S(2)}, u32[]{:S(2)}) collective-permute-start(bf16[4,4096]{1,0:T(4,128)(2,1)} %p_ref.1), channel_id=1, source_target_pairs={{0,26},{2,24},{4,30},{6,28},{8,18},{10,16},{12,22},{14,20},{16,10}... | collective-permute-start | bytes 98312 | tf_op jit(solution)/shard_map/ppermute | solution.py:27
  5.8 0.2 collective-permute-start
  6.1 0.2 collective-permute-done.2
  6.3 3.4 %collective-permute-done.3 = bf16[4,4096]{1,0:T(4,128)(2,1)S(1)} collective-permute-done((bf16[4,4096]{1,0:T(4,128)(2,1)}, bf16[4,4096]{1,0:T(4,128)(2,1)S(1)}, u32[]{:S(2)}, u32[]{:S(2)}) %collective-permute-start.3) | collective-permute-done | bytes 32800 | tf_op jit(solution)/shard_map/ppermute | solution.py:27
  9.7 2.0 %collective-permute-start.7 = (bf16[8,4096]{1,0:T(8,128)(2,1)S(1)}, bf16[8,4096]{1,0:T(8,128)(2,1)S(1)}, u32[]{:S(2)}, u32[]{:S(2)}) collective-permute-start(bf16[8,4096]{1,0:T(8,128)(2,1)S(1)} %pad_maximum_fusion.1.refs_1_), channel_id=1, source_target_pairs={{0,6},{2,4},{4,2},{6,0},{8,14},{10,12},{12,10},{14,8},{16,22},{18,... | collective-permute-start | bytes 196616 | tf_op jit(solution)/shard_map/ppermute | solution.py:27
  11.7 0.0 collective-permute-done
  11.7 0.8 %pad_maximum_fusion.refs_0_ = bf16[8,4096]{1,0:T(8,128)(2,1)S(1)} fusion(bf16[4,4096]{1,0:T(4,128)(2,1)S(1)} %collective-permute-done, bf16[4,4096]{1,0:T(4,128)(2,1)} %p_ref.1), kind=kLoop, calls=%fused_computation.6 | loop fusion | flops 131072 | bytes 131072 | tf_op jit(solution)/shard_map/concatenate | solution.py:167
  12.5 0.1 collective-permute-start.5
  12.6 0.6 %collective-permute-start.4 = (bf16[8,4096]{1,0:T(8,128)(2,1)S(1)}, bf16[8,4096]{1,0:T(8,128)(2,1)S(1)}, u32[]{:S(2)}, u32[]{:S(2)}) collective-permute-start(bf16[8,4096]{1,0:T(8,128)(2,1)S(1)} %pad_maximum_fusion.1.refs_1_), channel_id=1, source_target_pairs={{0,2},{2,0},{4,6},{6,4},{8,10},{10,8},{12,14},{14,12},{16,18},{18,... | collective-permute-start | bytes 196616 | tf_op jit(solution)/shard_map/ppermute | solution.py:27
  13.2 0.0 collective-permute-start.1
  13.2 0.5 %collective-permute-done.7.refs_3_ = bf16[8,4096]{1,0:T(8,128)(2,1)S(1)} collective-permute-done((bf16[8,4096]{1,0:T(8,128)(2,1)S(1)}, bf16[8,4096]{1,0:T(8,128)(2,1)S(1)}, u32[]{:S(2)}, u32[]{:S(2)}) %collective-permute-start.7) | collective-permute-done | bytes 65568 | tf_op jit(solution)/shard_map/ppermute | solution.py:27
  13.7 0.6 %collective-permute-start.8 = (bf16[8,4096]{1,0:T(8,128)(2,1)S(1)}, bf16[8,4096]{1,0:T(8,128)(2,1)S(1)}, u32[]{:S(2)}, u32[]{:S(2)}) collective-permute-start(bf16[8,4096]{1,0:T(8,128)(2,1)S(1)} %collective-permute-done.7.refs_3_), channel_id=1, source_target_pairs={{0,2},{2,0},{4,6},{6,4},{8,10},{10,8},{12,14},{14,12},{16,18},{18,... | collective-permute-start | bytes 196616 | tf_op jit(solution)/shard_map/ppermute | solution.py:27
  14.3 2.6 %collective-permute-done.5.refs_2_ = bf16[8,4096]{1,0:T(8,128)(2,1)S(1)} collective-permute-done((bf16[8,4096]{1,0:T(8,128)(2,1)S(1)}, bf16[8,4096]{1,0:T(8,128)(2,1)S(1)}, u32[]{:S(2)}, u32[]{:S(2)}) %collective-permute-start.5) | collective-permute-done | bytes 65568 | tf_op jit(solution)/shard_map/ppermute | solution.py:27
  16.8 0.0 collective-permute-start.6
  16.8 0.0 copy-start.3
  16.8 0.0 copy-start.4
  16.8 2.7 %prepare.1 = (f32[64,256]{1,0:T(8,128)}, f32[1,256]{1,0:T(1,128)}) custom-call(s32[1]{0:T(128)} %bitcast.me_ref.refs_4_, s32[32,256]{1,0:T(8,128)} %bitcast.9, s32[32,256]{1,0:T(8,128)} %bitcast.10, s32[1,256]{1,0:T(1,128)} %bitcast.11, bf16[256,4096]{1,0:T(8,128)(2,1)} %q_ref.1), custom_call_target="tpu_custom_call" | custom-call | flops 10000000 | bytes 3000000 | tf_op jit(solution)/shard_map/prepare/pallas_call | solution.py:178
  19.5 0.0 copy-done
  19.5 0.0 copy-start.2
  19.5 0.0 copy-start.5
  19.5 0.7 %first_scores.1 = (f32[32,256]{1,0:T(8,128)S(1)}, f32[32,128]{1,0:T(8,128)S(1)}) custom-call(bf16[8,4096]{1,0:T(8,128)(2,1)S(1)} %pad_maximum_fusion.refs_0_, bf16[8,4096]{1,0:T(8,128)(2,1)S(1)} %pad_maximum_fusion.1.refs_1_, bf16[8,4096]{1,0:T(8,128)(2,1)S(1)} %collective-permute-done.5.refs_2_, bf16[8,4096]{1,0:T(8,128)(2,1)S(1)} %collective-permute-done.7.refs_3_, ...), custom_call_target="tpu_custom_call" | custom-call | flops 67108864 | bytes 2000000 | tf_op jit(solution)/shard_map/first_scores/pallas_call | solution.py:197
  20.3 0.0 collective-permute-done.4.refs_1_.refs_5_
  20.3 0.0 collective-permute-done.1.refs_0_.refs_4_
  20.3 0.0 collective-permute-done.8.refs_3_.refs_7_
  20.3 0.0 collective-permute-done.6.refs_2_.refs_6_
  20.3 0.0 copy-done.3
  20.3 0.0 copy-done.4
  20.3 0.0 copy-done.2
  20.4 0.0 copy-done.5
  20.4 1.6 %loss.1 = (bf16[32,4096]{1,0:T(8,128)(2,1)S(1)}, bf16[32,256]{1,0:T(8,128)(2,1)S(1)}, bf16[64,256]{1,0:T(8,128)(2,1)S(1)}, f32[1,256]{1,0:T(1,128)}, f32[1,256]{1,0:T(1,128)S(1)}) custom-call(bf16[8,4096]{1,0:T(8,128)(2,1)S(1)} %collective-permute-done.1.refs_0_.refs_4_, bf16[8,4096]{1,0:T(8,128)(2,1)S(1)} %collective-permute-done.4.refs_1_.refs_5_, ...), custom_call_target="tpu_custom_call" | custom-call | flops 134217728 | bytes 2000000 | tf_op jit(solution)/shard_map/loss/pallas_call | solution.py:206
  22.0 0.6 %collective-permute-start.9 = (bf16[32,4096]{1,0:T(8,128)(2,1)S(1)}, bf16[32,4096]{1,0:T(8,128)(2,1)S(1)}, u32[]{:S(2)}, u32[]{:S(2)}) collective-permute-start(bf16[32,4096]{1,0:T(8,128)(2,1)S(1)} %get-tuple-element.20), channel_id=1, source_target_pairs={{0,2},{2,0},{4,6},{6,4},{8,10},{10,8},{12,14},{14,12},{16,18},{18,... | collective-permute-start | bytes 786440 | tf_op jit(solution)/shard_map/ppermute | solution.py:27
  22.5 0.5 %kept_terms.1 = f32[32,4096]{1,0:T(8,128)S(1)} custom-call(bf16[32,256]{1,0:T(8,128)(2,1)S(1)} %get-tuple-element.19.pa_ref, bf16[256,4096]{1,0:T(8,128)(2,1)S(1)} %copy-done), custom_call_target="tpu_custom_call" | custom-call | flops 67108864 | bytes 2000000 | tf_op jit(solution)/shard_map/kept_terms/pallas_call | solution.py:221
  23.0 0.7 %collective-permute-done.9 = bf16[32,4096]{1,0:T(8,128)(2,1)S(1)} collective-permute-done((bf16[32,4096]{1,0:T(8,128)(2,1)S(1)}, bf16[32,4096]{1,0:T(8,128)(2,1)S(1)}, u32[]{:S(2)}, u32[]{:S(2)}) %collective-permute-start.9) | collective-permute-done | bytes 262176 | tf_op jit(solution)/shard_map/ppermute | solution.py:27
  23.8 0.6 %collective-permute-start.10 = (bf16[16,4096]{1,0:T(8,128)(2,1)S(1)}, bf16[16,4096]{1,0:T(8,128)(2,1)S(1)}, u32[]{:S(2)}, u32[]{:S(2)}) collective-permute-start(bf16[16,4096]{1,0:T(8,128)(2,1)S(1)} %slice.41), channel_id=1, source_target_pairs={{0,6},{2,4},{4,2},{6,0},{8,14},{10,12},{12,10},{14,8},{16,22},{18,... | collective-permute-start | bytes 393224 | tf_op jit(solution)/shard_map/ppermute | solution.py:27
  24.4 4.7 %collective-permute-done.10 = bf16[16,4096]{1,0:T(8,128)(2,1)S(1)} collective-permute-done((bf16[16,4096]{1,0:T(8,128)(2,1)S(1)}, bf16[16,4096]{1,0:T(8,128)(2,1)S(1)}, u32[]{:S(2)}, u32[]{:S(2)}) %collective-permute-start.10) | collective-permute-done | bytes 131104 | tf_op jit(solution)/shard_map/ppermute | solution.py:27
  29.2 1.1 %collective-permute-start.11 = (bf16[4,4096]{1,0:T(4,128)(2,1)S(1)}, bf16[4,4096]{1,0:T(4,128)(2,1)S(1)}, u32[]{:S(2)}, u32[]{:S(2)}) collective-permute-start(bf16[4,4096]{1,0:T(4,128)(2,1)S(1)} %get-tuple-element.25), channel_id=1, source_target_pairs={{0,26},{2,24},{4,30},{6,28},{8,18},{10,16},{12,22},{14,20},{16,10}... | collective-permute-start | bytes 98312 | tf_op jit(solution)/shard_map/ppermute | solution.py:27
  30.3 0.6 %collective-permute-start.13 = (bf16[4,4096]{1,0:T(4,128)(2,1)S(1)}, bf16[4,4096]{1,0:T(4,128)(2,1)S(1)}, u32[]{:S(2)}, u32[]{:S(2)}) collective-permute-start(bf16[4,4096]{1,0:T(4,128)(2,1)S(1)} %get-tuple-element.26), channel_id=1, source_target_pairs={{0,10},{2,8},{4,14},{6,12},{8,2},{10,0},{12,6},{14,4},{16,26},{18,... | collective-permute-start | bytes 98312 | tf_op jit(solution)/shard_map/ppermute | solution.py:27
  30.9 2.4 %collective-permute-start.12 = (bf16[4,4096]{1,0:T(4,128)(2,1)S(1)}, bf16[4,4096]{1,0:T(4,128)(2,1)S(1)}, u32[]{:S(2)}, u32[]{:S(2)}) collective-permute-start(bf16[4,4096]{1,0:T(4,128)(2,1)S(1)} %get-tuple-element.27), channel_id=1, source_target_pairs={{0,18},{2,16},{4,22},{6,20},{8,26},{10,24},{12,30},{14,28},{16,2},... | collective-permute-start | bytes 98312 | tf_op jit(solution)/shard_map/ppermute | solution.py:27
  33.3 1.2 %collective-permute-done.11 = bf16[4,4096]{1,0:T(4,128)(2,1)S(1)} collective-permute-done((bf16[4,4096]{1,0:T(4,128)(2,1)S(1)}, bf16[4,4096]{1,0:T(4,128)(2,1)S(1)}, u32[]{:S(2)}, u32[]{:S(2)}) %collective-permute-start.11) | collective-permute-done | bytes 32800 | tf_op jit(solution)/shard_map/ppermute | solution.py:27
  34.5 0.0 collective-permute-done.13
  34.5 1.1 %collective-permute-done.12 = bf16[4,4096]{1,0:T(4,128)(2,1)S(1)} collective-permute-done((bf16[4,4096]{1,0:T(4,128)(2,1)S(1)}, bf16[4,4096]{1,0:T(4,128)(2,1)S(1)}, u32[]{:S(2)}, u32[]{:S(2)}) %collective-permute-start.12) | collective-permute-done | bytes 32800 | tf_op jit(solution)/shard_map/ppermute | solution.py:27
  35.6 1.6 %collective-permute-start.14 = (bf16[4,4096]{1,0:T(4,128)(2,1)S(1)}, bf16[4,4096]{1,0:T(4,128)(2,1)S(1)}, u32[]{:S(2)}, u32[]{:S(2)}) collective-permute-start(bf16[4,4096]{1,0:T(4,128)(2,1)S(1)} %get-tuple-element.21), channel_id=1, source_target_pairs={{0,1},{1,0},{2,3},{3,2},{4,5},{5,4},{6,7},{7,6},{8,9},{9,8},{10,11... | collective-permute-start | bytes 98312 | tf_op jit(solution)/shard_map/ppermute | solution.py:27
  37.2 4.1 %query_gradients.1 = bf16[256,4096]{1,0:T(8,128)(2,1)} custom-call(bf16[8,4096]{1,0:T(8,128)(2,1)S(1)} %pad_maximum_fusion.refs_0_, bf16[8,4096]{1,0:T(8,128)(2,1)S(1)} %pad_maximum_fusion.1.refs_1_, bf16[8,4096]{1,0:T(8,128)(2,1)S(1)} %collective-permute-done.5.refs_2_, bf16[8,4096]{1,0:T(8,128)(2,1)S(1)} %collective-permute-done.7.refs_3_, ...), custom_call_target="tpu_custom_call" | custom-call | flops 134217728 | bytes 5000000 | tf_op jit(solution)/shard_map/query_gradients/pallas_call | solution.py:248
  41.3 0.0 collective-permute-done.14.refs_0_
  41.3 0.0 copy-done.1
  41.3 0.9 %passage_gradients.1 = bf16[4,4096]{1,0:T(4,128)(2,1)} custom-call(bf16[4,4096]{1,0:T(4,128)(2,1)S(1)} %copy-done.1, f32[4,4096]{1,0:T(4,128)S(1)} %get-tuple-element.22.total_ref, bf16[4,4096]{1,0:T(4,128)(2,1)S(1)} %collective-permute-done.14.refs_0_), custom_call_target="tpu_custom_call" | custom-call | flops 1000000 | bytes 200000 | tf_op jit(solution)/shard_map/passage_gradients/pallas_call | solution.py:258
  (7 shorter events, 0.2 us)
Async XLA Ops:
  0.6 18.9 %copy-start = (bf16[256,4096]{1,0:T(8,128)(2,1)S(1)}, bf16[256,4096]{1,0:T(8,128)(2,1)}, u32[]{:S(2)}) copy-start(bf16[256,4096]{1,0:T(8,128)(2,1)} %q_ref.1) | copy-start | bytes 6291460
  0.6 5.7 %collective-permute-start.2 = (bf16[4,4096]{1,0:T(4,128)(2,1)}, bf16[4,4096]{1,0:T(4,128)(2,1)S(1)}, u32[]{:S(2)}, u32[]{:S(2)}) collective-permute-start(bf16[4,4096]{1,0:T(4,128)(2,1)} %p_ref.1), channel_id=1, source_target_pairs={{0,18},{2,16},{4,22},{6,20},{8,26},{10,24},{12,30},{14,28},{16,2},... | collective-permute-start | bytes 98312 | tf_op jit(solution)/shard_map/ppermute | solution.py:27
  4.2 5.4 %collective-permute-start.3 = (bf16[4,4096]{1,0:T(4,128)(2,1)}, bf16[4,4096]{1,0:T(4,128)(2,1)S(1)}, u32[]{:S(2)}, u32[]{:S(2)}) collective-permute-start(bf16[4,4096]{1,0:T(4,128)(2,1)} %p_ref.1), channel_id=1, source_target_pairs={{0,26},{2,24},{4,30},{6,28},{8,18},{10,16},{12,22},{14,20},{16,10}... | collective-permute-start | bytes 98312 | tf_op jit(solution)/shard_map/ppermute | solution.py:27
  5.8 5.9 %collective-permute-start = (bf16[4,4096]{1,0:T(4,128)(2,1)}, bf16[4,4096]{1,0:T(4,128)(2,1)S(1)}, u32[]{:S(2)}, u32[]{:S(2)}) collective-permute-start(bf16[4,4096]{1,0:T(4,128)(2,1)} %p_ref.1), channel_id=1, source_target_pairs={{0,10},{2,8},{4,14},{6,12},{8,2},{10,0},{12,6},{14,4},{16,26},{18,... | collective-permute-start | bytes 98312 | tf_op jit(solution)/shard_map/ppermute | solution.py:27
  9.7 4.0 %collective-permute-start.7 = (bf16[8,4096]{1,0:T(8,128)(2,1)S(1)}, bf16[8,4096]{1,0:T(8,128)(2,1)S(1)}, u32[]{:S(2)}, u32[]{:S(2)}) collective-permute-start(bf16[8,4096]{1,0:T(8,128)(2,1)S(1)} %pad_maximum_fusion.1.refs_1_), channel_id=1, source_target_pairs={{0,6},{2,4},{4,2},{6,0},{8,14},{10,12},{12,10},{14,8},{16,22},{18,... | collective-permute-start | bytes 196616 | tf_op jit(solution)/shard_map/ppermute | solution.py:27
  12.5 4.3 %collective-permute-start.5 = (bf16[8,4096]{1,0:T(8,128)(2,1)S(1)}, bf16[8,4096]{1,0:T(8,128)(2,1)S(1)}, u32[]{:S(2)}, u32[]{:S(2)}) collective-permute-start(bf16[8,4096]{1,0:T(8,128)(2,1)S(1)} %pad_maximum_fusion.refs_0_), channel_id=1, source_target_pairs={{0,6},{2,4},{4,2},{6,0},{8,14},{10,12},{12,10},{14,8},{16,22},{18,... | collective-permute-start | bytes 196616 | tf_op jit(solution)/shard_map/ppermute | solution.py:27
  12.6 7.7 %collective-permute-start.4 = (bf16[8,4096]{1,0:T(8,128)(2,1)S(1)}, bf16[8,4096]{1,0:T(8,128)(2,1)S(1)}, u32[]{:S(2)}, u32[]{:S(2)}) collective-permute-start(bf16[8,4096]{1,0:T(8,128)(2,1)S(1)} %pad_maximum_fusion.1.refs_1_), channel_id=1, source_target_pairs={{0,2},{2,0},{4,6},{6,4},{8,10},{10,8},{12,14},{14,12},{16,18},{18,... | collective-permute-start | bytes 196616 | tf_op jit(solution)/shard_map/ppermute | solution.py:27
  13.2 7.1 %collective-permute-start.1 = (bf16[8,4096]{1,0:T(8,128)(2,1)S(1)}, bf16[8,4096]{1,0:T(8,128)(2,1)S(1)}, u32[]{:S(2)}, u32[]{:S(2)}) collective-permute-start(bf16[8,4096]{1,0:T(8,128)(2,1)S(1)} %pad_maximum_fusion.refs_0_), channel_id=1, source_target_pairs={{0,2},{2,0},{4,6},{6,4},{8,10},{10,8},{12,14},{14,12},{16,18},{18,... | collective-permute-start | bytes 196616 | tf_op jit(solution)/shard_map/ppermute | solution.py:27
  13.7 6.6 %collective-permute-start.8 = (bf16[8,4096]{1,0:T(8,128)(2,1)S(1)}, bf16[8,4096]{1,0:T(8,128)(2,1)S(1)}, u32[]{:S(2)}, u32[]{:S(2)}) collective-permute-start(bf16[8,4096]{1,0:T(8,128)(2,1)S(1)} %collective-permute-done.7.refs_3_), channel_id=1, source_target_pairs={{0,2},{2,0},{4,6},{6,4},{8,10},{10,8},{12,14},{14,12},{16,18},{18,... | collective-permute-start | bytes 196616 | tf_op jit(solution)/shard_map/ppermute | solution.py:27
  16.8 3.5 %collective-permute-start.6 = (bf16[8,4096]{1,0:T(8,128)(2,1)S(1)}, bf16[8,4096]{1,0:T(8,128)(2,1)S(1)}, u32[]{:S(2)}, u32[]{:S(2)}) collective-permute-start(bf16[8,4096]{1,0:T(8,128)(2,1)S(1)} %collective-permute-done.5.refs_2_), channel_id=1, source_target_pairs={{0,2},{2,0},{4,6},{6,4},{8,10},{10,8},{12,14},{14,12},{16,18},{18,... | collective-permute-start | bytes 196616 | tf_op jit(solution)/shard_map/ppermute | solution.py:27
  16.8 3.5 %copy-start.3 = (s32[256]{0:T(256)S(1)}, s32[256]{0:T(256)}, u32[]{:S(2)}) copy-start(s32[256]{0:T(256)} %param.9) | copy-start | bytes 3076
  16.8 3.5 %copy-start.4 = (f32[256]{0:T(256)S(1)}, f32[256]{0:T(256)}, u32[]{:S(2)}) copy-start(f32[256]{0:T(256)} %param.13) | copy-start | bytes 3076
  19.5 0.8 %copy-start.2 = (f32[64,256]{1,0:T(8,128)S(1)}, f32[64,256]{1,0:T(8,128)}, u32[]{:S(2)}) copy-start(f32[64,256]{1,0:T(8,128)} %get-tuple-element.14.refs_8_) | copy-start | bytes 196612
  19.5 0.8 %copy-start.5 = (f32[1,256]{1,0:T(1,128)S(1)}, f32[1,256]{1,0:T(1,128)}, u32[]{:S(2)}) copy-start(f32[1,256]{1,0:T(1,128)} %get-tuple-element.15.refs_9_) | copy-start | bytes 3076
  22.0 1.7 %collective-permute-start.9 = (bf16[32,4096]{1,0:T(8,128)(2,1)S(1)}, bf16[32,4096]{1,0:T(8,128)(2,1)S(1)}, u32[]{:S(2)}, u32[]{:S(2)}) collective-permute-start(bf16[32,4096]{1,0:T(8,128)(2,1)S(1)} %get-tuple-element.20), channel_id=1, source_target_pairs={{0,2},{2,0},{4,6},{6,4},{8,10},{10,8},{12,14},{14,12},{16,18},{18,... | collective-permute-start | bytes 786440 | tf_op jit(solution)/shard_map/ppermute | solution.py:27
  23.8 5.3 %collective-permute-start.10 = (bf16[16,4096]{1,0:T(8,128)(2,1)S(1)}, bf16[16,4096]{1,0:T(8,128)(2,1)S(1)}, u32[]{:S(2)}, u32[]{:S(2)}) collective-permute-start(bf16[16,4096]{1,0:T(8,128)(2,1)S(1)} %slice.41), channel_id=1, source_target_pairs={{0,6},{2,4},{4,2},{6,0},{8,14},{10,12},{12,10},{14,8},{16,22},{18,... | collective-permute-start | bytes 393224 | tf_op jit(solution)/shard_map/ppermute | solution.py:27
  29.2 5.3 %collective-permute-start.11 = (bf16[4,4096]{1,0:T(4,128)(2,1)S(1)}, bf16[4,4096]{1,0:T(4,128)(2,1)S(1)}, u32[]{:S(2)}, u32[]{:S(2)}) collective-permute-start(bf16[4,4096]{1,0:T(4,128)(2,1)S(1)} %get-tuple-element.25), channel_id=1, source_target_pairs={{0,26},{2,24},{4,30},{6,28},{8,18},{10,16},{12,22},{14,20},{16,10}... | collective-permute-start | bytes 98312 | tf_op jit(solution)/shard_map/ppermute | solution.py:27
  30.3 4.2 %collective-permute-start.13 = (bf16[4,4096]{1,0:T(4,128)(2,1)S(1)}, bf16[4,4096]{1,0:T(4,128)(2,1)S(1)}, u32[]{:S(2)}, u32[]{:S(2)}) collective-permute-start(bf16[4,4096]{1,0:T(4,128)(2,1)S(1)} %get-tuple-element.26), channel_id=1, source_target_pairs={{0,10},{2,8},{4,14},{6,12},{8,2},{10,0},{12,6},{14,4},{16,26},{18,... | collective-permute-start | bytes 98312 | tf_op jit(solution)/shard_map/ppermute | solution.py:27
  30.9 4.7 %collective-permute-start.12 = (bf16[4,4096]{1,0:T(4,128)(2,1)S(1)}, bf16[4,4096]{1,0:T(4,128)(2,1)S(1)}, u32[]{:S(2)}, u32[]{:S(2)}) collective-permute-start(bf16[4,4096]{1,0:T(4,128)(2,1)S(1)} %get-tuple-element.27), channel_id=1, source_target_pairs={{0,18},{2,16},{4,22},{6,20},{8,26},{10,24},{12,30},{14,28},{16,2},... | collective-permute-start | bytes 98312 | tf_op jit(solution)/shard_map/ppermute | solution.py:27
  35.6 5.7 %collective-permute-start.14 = (bf16[4,4096]{1,0:T(4,128)(2,1)S(1)}, bf16[4,4096]{1,0:T(4,128)(2,1)S(1)}, u32[]{:S(2)}, u32[]{:S(2)}) collective-permute-start(bf16[4,4096]{1,0:T(4,128)(2,1)S(1)} %get-tuple-element.21), channel_id=1, source_target_pairs={{0,1},{1,0},{2,3},{3,2},{4,5},{5,4},{6,7},{7,6},{8,9},{9,8},{10,11... | collective-permute-start | bytes 98312 | tf_op jit(solution)/shard_map/ppermute | solution.py:27
  37.2 4.1 %copy-start.1 = (bf16[4,4096]{1,0:T(4,128)(2,1)S(1)}, bf16[4,4096]{1,0:T(4,128)(2,1)}, u32[]{:S(2)}) copy-start(bf16[4,4096]{1,0:T(4,128)(2,1)} %p_ref.1) | copy-start | bytes 98308
where the time goes:
time: 42.4 us; the launch traced here: 42.2 us
  starting transfers between devices  15.6 us (37%)
  waiting for transfers between devices  14.3 us (34%)
  Pallas kernels  10.4 us (25%)
  other arithmetic  0.95 us (2%)
  between operations  0.77 us (2%)
    ppermute x15, starting transfers between devices, swap(): return lax.ppermute(x, axis, [(i, i ^ mask) for i in range(size)])  15.6 us
    ppermute x15, waiting for transfers between devices, swap(): return lax.ppermute(x, axis, [(i, i ^ mask) for i in range(size)])  14.3 us
    pallas_call x1, Pallas kernels, body(): pl.pallas_call(functools.partial(query_kernel, 2 * n), out_shape=jax.Shap...  4.11 us
    pallas_call x1, Pallas kernels, body(): pl.pallas_call(functools.partial(prepare_kernel, stages, block), out_shap...  2.66 us
    pallas_call x1, Pallas kernels, body(): pl.pallas_call(functools.partial(loss_kernel, n, stages, block), out_shap...  1.6 us
    pallas_call x1, Pallas kernels, body(): pl.pallas_call(functools.partial(passage_kernel, len(moved)), out_shape=j...  0.86 us
  transfers between devices with their start and end apart: 15, of which 8 were waited for; matrix products, arithmetic and copies ran while one was open for 2% of the time, Pallas kernels for 19%

commit v1 on v0

--- a/solution.py
+++ b/solution.py
@@ -128,14 +128,45 @@
     kept_ref[...] = jnp.dot(pa_ref[...], q_ref[...], preferred_element_type=jnp.float32)
 
 
-def query_kernel(n, *refs):
-    qc_ref, q_ref, inner_ref, out_ref = refs[n:]
+def split_kernel(total_ref, got_ref, kept0_ref, kept1_ref, sent0_ref, sent1_ref):
+    total = total_ref[...] + wide(got_ref[...])
+    part = kept0_ref.shape[0]
+    for k, ref in enumerate((kept0_ref, kept1_ref, sent0_ref, sent1_ref)):
+        ref[...] = total[k * part : (k + 1) * part].astype(ref.dtype)
+
+
+def far_kernel(kept_ref, got_ref, low_ref, high_ref):
+    total = kept_ref[...] + wide(got_ref[...])
+    part = low_ref.shape[0]
+    low_ref[...] = total[:part].astype(low_ref.dtype)
+    high_ref[...] = total[part:].astype(high_ref.dtype)
+
+
+def sum_call(kernel, outs, *args):
+    return pl.pallas_call(
+        kernel,
+        out_shape=tuple(jax.ShapeDtypeStruct(*out) for out in outs),
+        in_specs=[VMEM] * len(args),
+        out_specs=(VMEM,) * len(outs),
+        cost_estimate=cost(200000, 1000000),
+        compiler_params=LIMIT,
+    )(*args)
+
+
+def query_kernel(n, first, *refs):
+    qc_ref, q_ref, inner_ref = refs[n : n + 3]
+    out_ref, coef_ref, column_ref = refs[-3:]
     step = out_ref.shape[1]
-    at = pl.ds(pl.multiple_of(pl.program_id(0) * step, step), step)
+
+    @pl.when(pl.program_id(0) == 0)
+    def _():
+        coef_ref[...] = qc_ref[...].T
+        column_ref[...] = jnp.broadcast_to(inner_ref[...], (128, inner_ref.shape[1])).T
+
+    at = pl.ds(pl.multiple_of((first + pl.program_id(0)) * step, step), step)
     rows = jnp.concatenate([r[:, at] for r in refs[:n]], axis=0)
-    qdir = lax.dot_general(qc_ref[...], rows, (((0,), (0,)), ((), ())), preferred_element_type=jnp.float32)
-    inner = jnp.broadcast_to(inner_ref[...], (128, inner_ref.shape[1])).T[:, :1]
-    out_ref[...] = (qdir - wide(q_ref[:, at]) * inner).astype(jnp.bfloat16)
+    qdir = jnp.dot(coef_ref[...], rows, preferred_element_type=jnp.float32)
+    out_ref[...] = (qdir - wide(q_ref[:, at]) * column_ref[:, :1]).astype(jnp.bfloat16)
 
 
 def passage_kernel(n, p_ref, total_ref, *refs):
@@ -164,7 +195,9 @@
         pool_size = loop * block
 
         first = [passages] + [swap(passages, "loop", loop, m) for m in stages[0][1:]]
-        pool = [jnp.concatenate(first[k : k + 2], axis=0) for k in (0, 2)]
+        pool = []
+        for k in (0, 2):
+            pool.append(jnp.concatenate(first[k : k + 2], axis=0))
         for at, (_, m) in enumerate(stages[1:]):
             moved = [swap(t, "loop", loop, m) for t in pool]
             pool = pool + moved
@@ -228,16 +261,25 @@
             name="kept_terms",
         )(pa, queries)
 
-        total = total + wide(swap(sent, "loop", loop, stages[-1][1]))
-        for masks in stages[:-1][::-1]:
-            part = total.shape[0] // len(masks)
-            moved = [
-                swap(total[k * part : (k + 1) * part].astype(jnp.bfloat16), "loop", loop, masks[k])
-                for k in range(len(masks) - 1, 0, -1)
-            ]
+        received = swap(sent, "loop", loop, stages[-1][1])
+        for _, m in stages[2:-1][::-1]:
+            total = total + wide(received)
+            part = total.shape[0] // 2
+            received = swap(total[part:].astype(jnp.bfloat16), "loop", loop, m)
             total = total[:part]
-            for t in moved:
-                total = total + wide(t)
+        part = total.shape[0] // 4
+        kept0, kept1, sent0, sent1 = sum_call(
+            split_kernel, [((part, width), f32)] * 2 + [((part, width), jnp.bfloat16)] * 2, total, received
+        )
+        got1 = swap(sent1, "loop", loop, stages[1][1])
+        got0 = swap(sent0, "loop", loop, stages[1][1])
+        term = ((block, width), jnp.bfloat16)
+        far2, far3 = sum_call(far_kernel, [term, term], kept1, got1)
+        got3 = swap(far3, "loop", loop, stages[0][3])
+        got2 = swap(far2, "loop", loop, stages[0][2])
+        total, far1 = sum_call(far_kernel, [((block, width), f32), term], kept0, got0)
+        got1 = swap(far1, "loop", loop, stages[0][1])
+        total = total + wide(got1) + wide(got2) + wide(got3)
         moved = []
         for b in range(narrow.bit_length() - 1):
             if moved:
@@ -245,16 +287,22 @@
             moved.append(swap(total.astype(jnp.bfloat16), "narrow", narrow, 1 << b))
 
         step = 512
-        grad_queries = pl.pallas_call(
-            functools.partial(query_kernel, 2 * n),
-            out_shape=jax.ShapeDtypeStruct(queries.shape, jnp.bfloat16),
-            grid=(width // step,),
-            in_specs=[VMEM] * (2 * n + 3),
-            out_specs=pl.BlockSpec((count, step), lambda i: (0, i)),
-            cost_estimate=cost(2 * pool_size * count * width, 5000000),
-            compiler_params=LIMIT,
-            name="query_gradients",
-        )(*pool, qc, queries, inner)
+        calls = 2
+        steps = width // step // calls
+        grad_queries = None
+        for k in range(calls):
+            before = [] if grad_queries is None else [grad_queries]
+            grad_queries = pl.pallas_call(
+                functools.partial(query_kernel, 2 * n, k * steps),
+                out_shape=jax.ShapeDtypeStruct(queries.shape, jnp.bfloat16),
+                grid=(steps,),
+                in_specs=[VMEM] * (2 * n + 3) + [pl.BlockSpec(memory_space=pl.ANY)] * len(before),
+                out_specs=pl.BlockSpec((count, step), lambda i, k=k: (0, i + k * steps)),
+                input_output_aliases={2 * n + 3: 0} if before else {},
+                scratch_shapes=[pltpu.VMEM((count, pool_size), jnp.bfloat16), pltpu.VMEM((count, 128), f32)],
+                cost_estimate=cost(2 * pool_size * count * width // calls, 5000000 // calls),
+                compiler_params=LIMIT,
+            )(*pool, qc, queries, inner, *before)
         grad_passages = pl.pallas_call(
             functools.partial(passage_kernel, len(moved)),
             out_shape=jax.ShapeDtypeStruct(passages.shape, jnp.bfloat16),

time: 42.4 us -> 42.6 us (level)
  starting transfers between devices: 15.6 us -> 17.1 us
  waiting for transfers between devices: 14.3 us -> 12.8 us
    ppermute x15 -> x16, waiting for transfers between devices: 14.3 us -> 12.8 us  [swap(): return lax.ppermute(x, axis, [(i, i ^ mask) for i in range(size)])]
    ppermute x15 -> x16, starting transfers between devices: 15.6 us -> 17.1 us  [swap(): return lax.ppermute(x, axis, [(i, i ^ mask) for i in range(size)])]
    pallas_call x1 -> x5, Pallas kernels: 4.11 us -> 4.44 us  [the longest x2 4.36 us: body(): pl.pallas_call(functools.partial(query_kernel, 2 * n, k * steps), out_sha...]
  transfers between devices with their start and end apart: 15 -> 16, of which waited for: 8 -> 9; matrix products, arithmetic and copies ran while one was open for 2% -> 2% of each run, Pallas kernels for 19% -> 19%
where the time goes in v1:
time: 42.6 us; the launch traced here: 42.3 us
  starting transfers between devices  17.1 us (40%)
  waiting for transfers between devices  12.8 us (30%)
  Pallas kernels  10.7 us (25%)
  other arithmetic  0.87 us (2%)
  between operations  0.75 us (2%)
    ppermute x16, starting transfers between devices, swap(): return lax.ppermute(x, axis, [(i, i ^ mask) for i in range(size)])  17.1 us
    ppermute x16, waiting for transfers between devices, swap(): return lax.ppermute(x, axis, [(i, i ^ mask) for i in range(size)])  12.8 us
    pallas_call x2, Pallas kernels, body(): pl.pallas_call(functools.partial(query_kernel, 2 * n, k * steps), out_sha...  4.36 us
    pallas_call x1, Pallas kernels, body(): pl.pallas_call(functools.partial(prepare_kernel, stages, block), out_shap...  2.66 us
    pallas_call x1, Pallas kernels, body(): pl.pallas_call(functools.partial(loss_kernel, n, stages, block), out_shap...  1.6 us
    pallas_call x1, Pallas kernels, body(): pl.pallas_call(functools.partial(passage_kernel, len(moved)), out_shape=j...  0.86 us
  transfers between devices with their start and end apart: 16, of which 9 were waited for; matrix products, arithmetic and copies ran while one was open for 2% of the time, Pallas kernels for 19%

profile of v1, /device:TPU:0, one launch (start us, length us, event | category | flops | bytes accessed | tf_op | source)
XLA Modules:
  0.0 42.3 jit_solution(2236205810037861147)
XLA Ops:
  0.6 0.0 copy-start
  0.6 3.6 %collective-permute-start.2 = (bf16[4,4096]{1,0:T(4,128)(2,1)}, bf16[4,4096]{1,0:T(4,128)(2,1)S(1)}, u32[]{:S(2)}, u32[]{:S(2)}) collective-permute-start(bf16[4,4096]{1,0:T(4,128)(2,1)} %p_ref.1), channel_id=1, source_target_pairs={{0,18},{2,16},{4,22},{6,20},{8,26},{10,24},{12,30},{14,28},{16,2},... | collective-permute-start | bytes 98312 | tf_op jit(solution)/shard_map/ppermute | solution.py:27
  4.2 1.6 %collective-permute-start.3 = (bf16[4,4096]{1,0:T(4,128)(2,1)}, bf16[4,4096]{1,0:T(4,128)(2,1)S(1)}, u32[]{:S(2)}, u32[]{:S(2)}) collective-permute-start(bf16[4,4096]{1,0:T(4,128)(2,1)} %p_ref.1), channel_id=1, source_target_pairs={{0,26},{2,24},{4,30},{6,28},{8,18},{10,16},{12,22},{14,20},{16,10}... | collective-permute-start | bytes 98312 | tf_op jit(solution)/shard_map/ppermute | solution.py:27
  5.8 0.2 collective-permute-start
  6.1 0.2 collective-permute-done.2
  6.3 3.4 %collective-permute-done.3 = bf16[4,4096]{1,0:T(4,128)(2,1)S(1)} collective-permute-done((bf16[4,4096]{1,0:T(4,128)(2,1)}, bf16[4,4096]{1,0:T(4,128)(2,1)S(1)}, u32[]{:S(2)}, u32[]{:S(2)}) %collective-permute-start.3) | collective-permute-done | bytes 32800 | tf_op jit(solution)/shard_map/ppermute | solution.py:27
  9.7 2.0 %collective-permute-start.7 = (bf16[8,4096]{1,0:T(8,128)(2,1)S(1)}, bf16[8,4096]{1,0:T(8,128)(2,1)S(1)}, u32[]{:S(2)}, u32[]{:S(2)}) collective-permute-start(bf16[8,4096]{1,0:T(8,128)(2,1)S(1)} %pad_maximum_fusion.1.refs_1_), channel_id=1, source_target_pairs={{0,6},{2,4},{4,2},{6,0},{8,14},{10,12},{12,10},{14,8},{16,22},{18,... | collective-permute-start | bytes 196616 | tf_op jit(solution)/shard_map/ppermute | solution.py:27
  11.7 0.0 collective-permute-done
  11.7 0.8 %pad_maximum_fusion.refs_0_ = bf16[8,4096]{1,0:T(8,128)(2,1)S(1)} fusion(bf16[4,4096]{1,0:T(4,128)(2,1)S(1)} %collective-permute-done, bf16[4,4096]{1,0:T(4,128)(2,1)} %p_ref.1), kind=kLoop, calls=%fused_computation | loop fusion | flops 131072 | bytes 131072 | tf_op jit(solution)/shard_map/concatenate | solution.py:200
  12.5 0.1 collective-permute-start.5
  12.6 0.6 %collective-permute-start.4 = (bf16[8,4096]{1,0:T(8,128)(2,1)S(1)}, bf16[8,4096]{1,0:T(8,128)(2,1)S(1)}, u32[]{:S(2)}, u32[]{:S(2)}) collective-permute-start(bf16[8,4096]{1,0:T(8,128)(2,1)S(1)} %pad_maximum_fusion.1.refs_1_), channel_id=1, source_target_pairs={{0,2},{2,0},{4,6},{6,4},{8,10},{10,8},{12,14},{14,12},{16,18},{18,... | collective-permute-start | bytes 196616 | tf_op jit(solution)/shard_map/ppermute | solution.py:27
  13.2 0.0 collective-permute-start.1
  13.2 0.5 %collective-permute-done.7.refs_3_ = bf16[8,4096]{1,0:T(8,128)(2,1)S(1)} collective-permute-done((bf16[8,4096]{1,0:T(8,128)(2,1)S(1)}, bf16[8,4096]{1,0:T(8,128)(2,1)S(1)}, u32[]{:S(2)}, u32[]{:S(2)}) %collective-permute-start.7) | collective-permute-done | bytes 65568 | tf_op jit(solution)/shard_map/ppermute | solution.py:27
  13.7 0.6 %collective-permute-start.8 = (bf16[8,4096]{1,0:T(8,128)(2,1)S(1)}, bf16[8,4096]{1,0:T(8,128)(2,1)S(1)}, u32[]{:S(2)}, u32[]{:S(2)}) collective-permute-start(bf16[8,4096]{1,0:T(8,128)(2,1)S(1)} %collective-permute-done.7.refs_3_), channel_id=1, source_target_pairs={{0,2},{2,0},{4,6},{6,4},{8,10},{10,8},{12,14},{14,12},{16,18},{18,... | collective-permute-start | bytes 196616 | tf_op jit(solution)/shard_map/ppermute | solution.py:27
  14.3 2.6 %collective-permute-done.5.refs_2_ = bf16[8,4096]{1,0:T(8,128)(2,1)S(1)} collective-permute-done((bf16[8,4096]{1,0:T(8,128)(2,1)S(1)}, bf16[8,4096]{1,0:T(8,128)(2,1)S(1)}, u32[]{:S(2)}, u32[]{:S(2)}) %collective-permute-start.5) | collective-permute-done | bytes 65568 | tf_op jit(solution)/shard_map/ppermute | solution.py:27
  16.8 0.0 collective-permute-start.6
  16.8 2.7 %prepare.1 = (f32[64,256]{1,0:T(8,128)}, f32[1,256]{1,0:T(1,128)}) custom-call(s32[1]{0:T(128)} %bitcast.me_ref.refs_4_, s32[32,256]{1,0:T(8,128)} %bitcast.9, s32[32,256]{1,0:T(8,128)} %bitcast.10, s32[1,256]{1,0:T(1,128)} %bitcast.11, bf16[256,4096]{1,0:T(8,128)(2,1)} %q_ref.1), custom_call_target="tpu_custom_call" | custom-call | flops 10000000 | bytes 3000000 | tf_op jit(solution)/shard_map/prepare/pallas_call | solution.py:211
  19.5 0.0 copy-done
  19.5 0.0 copy-start.2
  19.5 0.0 copy-start.5
  19.5 0.7 %first_scores.1 = (f32[32,256]{1,0:T(8,128)S(1)}, f32[32,128]{1,0:T(8,128)S(1)}) custom-call(bf16[8,4096]{1,0:T(8,128)(2,1)S(1)} %pad_maximum_fusion.refs_0_, bf16[8,4096]{1,0:T(8,128)(2,1)S(1)} %pad_maximum_fusion.1.refs_1_, bf16[8,4096]{1,0:T(8,128)(2,1)S(1)} %collective-permute-done.5.refs_2_, bf16[8,4096]{1,0:T(8,128)(2,1)S(1)} %collective-permute-done.7.refs_3_, ...), custom_call_target="tpu_custom_call" | custom-call | flops 67108864 | bytes 2000000 | tf_op jit(solution)/shard_map/first_scores/pallas_call | solution.py:230
  20.3 0.0 collective-permute-done.4.refs_1_.refs_5_
  20.3 0.0 collective-permute-done.1.refs_0_.refs_4_
  20.3 0.0 collective-permute-done.8.refs_3_.refs_7_
  20.3 0.0 collective-permute-done.6.refs_2_.refs_6_
  20.3 0.0 copy-done.3
  20.3 0.0 copy-done.4
  20.3 0.0 copy-done.2
  20.4 0.0 copy-done.5
  20.4 1.6 %loss.1 = (bf16[32,4096]{1,0:T(8,128)(2,1)S(1)}, bf16[32,256]{1,0:T(8,128)(2,1)S(1)}, bf16[64,256]{1,0:T(8,128)(2,1)S(1)}, f32[1,256]{1,0:T(1,128)}, f32[1,256]{1,0:T(1,128)S(1)}) custom-call(bf16[8,4096]{1,0:T(8,128)(2,1)S(1)} %collective-permute-done.1.refs_0_.refs_4_, bf16[8,4096]{1,0:T(8,128)(2,1)S(1)} %collective-permute-done.4.refs_1_.refs_5_, ...), custom_call_target="tpu_custom_call" | custom-call | flops 134217728 | bytes 2000000 | tf_op jit(solution)/shard_map/loss/pallas_call | solution.py:239
  22.0 0.6 %collective-permute-start.9 = (bf16[32,4096]{1,0:T(8,128)(2,1)S(1)}, bf16[32,4096]{1,0:T(8,128)(2,1)S(1)}, u32[]{:S(2)}, u32[]{:S(2)}) collective-permute-start(bf16[32,4096]{1,0:T(8,128)(2,1)S(1)} %get-tuple-element.28), channel_id=1, source_target_pairs={{0,2},{2,0},{4,6},{6,4},{8,10},{10,8},{12,14},{14,12},{16,18},{18,... | collective-permute-start | bytes 786440 | tf_op jit(solution)/shard_map/ppermute | solution.py:27
  22.5 0.5 %kept_terms.1.total_ref = f32[32,4096]{1,0:T(8,128)S(1)} custom-call(bf16[32,256]{1,0:T(8,128)(2,1)S(1)} %get-tuple-element.27.pa_ref, bf16[256,4096]{1,0:T(8,128)(2,1)S(1)} %copy-done), custom_call_target="tpu_custom_call" | custom-call | flops 67108864 | bytes 2000000 | tf_op jit(solution)/shard_map/kept_terms/pallas_call | solution.py:254
  23.0 0.7 %collective-permute-done.9.got_ref = bf16[32,4096]{1,0:T(8,128)(2,1)S(1)} collective-permute-done((bf16[32,4096]{1,0:T(8,128)(2,1)S(1)}, bf16[32,4096]{1,0:T(8,128)(2,1)S(1)}, u32[]{:S(2)}, u32[]{:S(2)}) %collective-permute-start.9) | collective-permute-done | bytes 262176 | tf_op jit(solution)/shard_map/ppermute | solution.py:27
  23.8 0.6 %collective-permute-start.10 = (bf16[8,4096]{1,0:T(8,128)(2,1)S(1)}, bf16[8,4096]{1,0:T(8,128)(2,1)S(1)}, u32[]{:S(2)}, u32[]{:S(2)}) collective-permute-start(bf16[8,4096]{1,0:T(8,128)(2,1)S(1)} %get-tuple-element.30), channel_id=1, source_target_pairs={{0,6},{2,4},{4,2},{6,0},{8,14},{10,12},{12,10},{14,8},{16,22},{18,... | collective-permute-start | bytes 196616 | tf_op jit(solution)/shard_map/ppermute | solution.py:27
  24.3 1.2 %collective-permute-start.12 = (bf16[8,4096]{1,0:T(8,128)(2,1)S(1)}, bf16[8,4096]{1,0:T(8,128)(2,1)S(1)}, u32[]{:S(2)}, u32[]{:S(2)}) collective-permute-start(bf16[8,4096]{1,0:T(8,128)(2,1)S(1)} %get-tuple-element.34), channel_id=1, source_target_pairs={{0,6},{2,4},{4,2},{6,0},{8,14},{10,12},{12,10},{14,8},{16,22},{18,... | collective-permute-start | bytes 196616 | tf_op jit(solution)/shard_map/ppermute | solution.py:27
  25.6 2.1 %collective-permute-done.10.got_ref = bf16[8,4096]{1,0:T(8,128)(2,1)S(1)} collective-permute-done((bf16[8,4096]{1,0:T(8,128)(2,1)S(1)}, bf16[8,4096]{1,0:T(8,128)(2,1)S(1)}, u32[]{:S(2)}, u32[]{:S(2)}) %collective-permute-start.10) | collective-permute-done | bytes 65568 | tf_op jit(solution)/shard_map/ppermute | solution.py:27
  27.7 0.7 %collective-permute-start.11 = (bf16[4,4096]{1,0:T(4,128)(2,1)S(1)}, bf16[4,4096]{1,0:T(4,128)(2,1)S(1)}, u32[]{:S(2)}, u32[]{:S(2)}) collective-permute-start(bf16[4,4096]{1,0:T(4,128)(2,1)S(1)} %get-tuple-element.32), channel_id=1, source_target_pairs={{0,10},{2,8},{4,14},{6,12},{8,2},{10,0},{12,6},{14,4},{16,26},{18,... | collective-permute-start | bytes 98312 | tf_op jit(solution)/shard_map/ppermute | solution.py:27
  28.4 0.7 %collective-permute-done.12.got_ref = bf16[8,4096]{1,0:T(8,128)(2,1)S(1)} collective-permute-done((bf16[8,4096]{1,0:T(8,128)(2,1)S(1)}, bf16[8,4096]{1,0:T(8,128)(2,1)S(1)}, u32[]{:S(2)}, u32[]{:S(2)}) %collective-permute-start.12) | collective-permute-done | bytes 65568 | tf_op jit(solution)/shard_map/ppermute | solution.py:27
  29.1 1.2 %collective-permute-start.13 = (bf16[4,4096]{1,0:T(4,128)(2,1)S(1)}, bf16[4,4096]{1,0:T(4,128)(2,1)S(1)}, u32[]{:S(2)}, u32[]{:S(2)}) collective-permute-start(bf16[4,4096]{1,0:T(4,128)(2,1)S(1)} %get-tuple-element.35), channel_id=1, source_target_pairs={{0,18},{2,16},{4,22},{6,20},{8,26},{10,24},{12,30},{14,28},{16,2},... | collective-permute-start | bytes 98312 | tf_op jit(solution)/shard_map/ppermute | solution.py:27
  30.3 2.5 %collective-permute-start.14 = (bf16[4,4096]{1,0:T(4,128)(2,1)S(1)}, bf16[4,4096]{1,0:T(4,128)(2,1)S(1)}, u32[]{:S(2)}, u32[]{:S(2)}) collective-permute-start(bf16[4,4096]{1,0:T(4,128)(2,1)S(1)} %get-tuple-element.36), channel_id=1, source_target_pairs={{0,26},{2,24},{4,30},{6,28},{8,18},{10,16},{12,22},{14,20},{16,10}... | collective-permute-start | bytes 98312 | tf_op jit(solution)/shard_map/ppermute | solution.py:27
  32.8 0.0 collective-permute-done.11
  32.8 0.6 %collective-permute-done.13 = bf16[4,4096]{1,0:T(4,128)(2,1)S(1)} collective-permute-done((bf16[4,4096]{1,0:T(4,128)(2,1)S(1)}, bf16[4,4096]{1,0:T(4,128)(2,1)S(1)}, u32[]{:S(2)}, u32[]{:S(2)}) %collective-permute-start.13) | collective-permute-done | bytes 32800 | tf_op jit(solution)/shard_map/ppermute | solution.py:27
  33.4 2.1 %collective-permute-done.14 = bf16[4,4096]{1,0:T(4,128)(2,1)S(1)} collective-permute-done((bf16[4,4096]{1,0:T(4,128)(2,1)S(1)}, bf16[4,4096]{1,0:T(4,128)(2,1)S(1)}, u32[]{:S(2)}, u32[]{:S(2)}) %collective-permute-start.14) | collective-permute-done | bytes 32800 | tf_op jit(solution)/shard_map/ppermute | solution.py:27
  35.5 1.6 %collective-permute-start.15 = (bf16[4,4096]{1,0:T(4,128)(2,1)S(1)}, bf16[4,4096]{1,0:T(4,128)(2,1)S(1)}, u32[]{:S(2)}, u32[]{:S(2)}) collective-permute-start(bf16[4,4096]{1,0:T(4,128)(2,1)S(1)} %get-tuple-element.37), channel_id=1, source_target_pairs={{0,1},{1,0},{2,3},{3,2},{4,5},{5,4},{6,7},{7,6},{8,9},{9,8},{10,11... | collective-permute-start | bytes 98312 | tf_op jit(solution)/shard_map/ppermute | solution.py:27
  37.1 2.2 %shard_map.94.refs_11_ = bf16[256,4096]{1,0:T(8,128)(2,1)} custom-call(bf16[8,4096]{1,0:T(8,128)(2,1)S(1)} %pad_maximum_fusion.refs_0_, bf16[8,4096]{1,0:T(8,128)(2,1)S(1)} %pad_maximum_fusion.1.refs_1_, bf16[8,4096]{1,0:T(8,128)(2,1)S(1)} %collective-permute-done.5.refs_2_, bf16[8,4096]{1,0:T(8,128)(2,1)S(1)} %collective-permute-done.7.refs_3_, ...), custom_call_target="tpu_custom_call" | custom-call | flops 67108864 | bytes 2500000 | tf_op jit(solution)/shard_map/pallas_call | solution.py:295
  39.3 2.2 %shard_map.95 = bf16[256,4096]{1,0:T(8,128)(2,1)} custom-call(bf16[8,4096]{1,0:T(8,128)(2,1)S(1)} %pad_maximum_fusion.refs_0_, bf16[8,4096]{1,0:T(8,128)(2,1)S(1)} %pad_maximum_fusion.1.refs_1_, bf16[8,4096]{1,0:T(8,128)(2,1)S(1)} %collective-permute-done.5.refs_2_, ...), custom_call_target="tpu_custom_call", output_to_operand_aliasing={{}: (11, {})} | custom-call | flops 67108864 | bytes 2500000 | tf_op jit(solution)/shard_map/pallas_call | solution.py:295
  41.4 0.0 collective-permute-done.15.refs_0_
  41.5 0.9 %passage_gradients.1 = bf16[4,4096]{1,0:T(4,128)(2,1)} custom-call(bf16[4,4096]{1,0:T(4,128)(2,1)S(1)} %copy-done.1, f32[4,4096]{1,0:T(4,128)S(1)} %get-tuple-element.38.total_ref, bf16[4,4096]{1,0:T(4,128)(2,1)S(1)} %collective-permute-done.15.refs_0_), custom_call_target="tpu_custom_call" | custom-call | flops 1000000 | bytes 200000 | tf_op jit(solution)/shard_map/passage_gradients/pallas_call | solution.py:306
  (9 shorter events, 0.2 us)
Async XLA Ops:
  0.6 18.9 %copy-start = (bf16[256,4096]{1,0:T(8,128)(2,1)S(1)}, bf16[256,4096]{1,0:T(8,128)(2,1)}, u32[]{:S(2)}) copy-start(bf16[256,4096]{1,0:T(8,128)(2,1)} %q_ref.1) | copy-start | bytes 6291460
  0.6 5.7 %collective-permute-start.2 = (bf16[4,4096]{1,0:T(4,128)(2,1)}, bf16[4,4096]{1,0:T(4,128)(2,1)S(1)}, u32[]{:S(2)}, u32[]{:S(2)}) collective-permute-start(bf16[4,4096]{1,0:T(4,128)(2,1)} %p_ref.1), channel_id=1, source_target_pairs={{0,18},{2,16},{4,22},{6,20},{8,26},{10,24},{12,30},{14,28},{16,2},... | collective-permute-start | bytes 98312 | tf_op jit(solution)/shard_map/ppermute | solution.py:27
  4.2 5.4 %collective-permute-start.3 = (bf16[4,4096]{1,0:T(4,128)(2,1)}, bf16[4,4096]{1,0:T(4,128)(2,1)S(1)}, u32[]{:S(2)}, u32[]{:S(2)}) collective-permute-start(bf16[4,4096]{1,0:T(4,128)(2,1)} %p_ref.1), channel_id=1, source_target_pairs={{0,26},{2,24},{4,30},{6,28},{8,18},{10,16},{12,22},{14,20},{16,10}... | collective-permute-start | bytes 98312 | tf_op jit(solution)/shard_map/ppermute | solution.py:27
  5.8 5.9 %collective-permute-start = (bf16[4,4096]{1,0:T(4,128)(2,1)}, bf16[4,4096]{1,0:T(4,128)(2,1)S(1)}, u32[]{:S(2)}, u32[]{:S(2)}) collective-permute-start(bf16[4,4096]{1,0:T(4,128)(2,1)} %p_ref.1), channel_id=1, source_target_pairs={{0,10},{2,8},{4,14},{6,12},{8,2},{10,0},{12,6},{14,4},{16,26},{18,... | collective-permute-start | bytes 98312 | tf_op jit(solution)/shard_map/ppermute | solution.py:27
  9.7 4.0 %collective-permute-start.7 = (bf16[8,4096]{1,0:T(8,128)(2,1)S(1)}, bf16[8,4096]{1,0:T(8,128)(2,1)S(1)}, u32[]{:S(2)}, u32[]{:S(2)}) collective-permute-start(bf16[8,4096]{1,0:T(8,128)(2,1)S(1)} %pad_maximum_fusion.1.refs_1_), channel_id=1, source_target_pairs={{0,6},{2,4},{4,2},{6,0},{8,14},{10,12},{12,10},{14,8},{16,22},{18,... | collective-permute-start | bytes 196616 | tf_op jit(solution)/shard_map/ppermute | solution.py:27
  12.5 4.3 %collective-permute-start.5 = (bf16[8,4096]{1,0:T(8,128)(2,1)S(1)}, bf16[8,4096]{1,0:T(8,128)(2,1)S(1)}, u32[]{:S(2)}, u32[]{:S(2)}) collective-permute-start(bf16[8,4096]{1,0:T(8,128)(2,1)S(1)} %pad_maximum_fusion.refs_0_), channel_id=1, source_target_pairs={{0,6},{2,4},{4,2},{6,0},{8,14},{10,12},{12,10},{14,8},{16,22},{18,... | collective-permute-start | bytes 196616 | tf_op jit(solution)/shard_map/ppermute | solution.py:27
  12.6 7.7 %collective-permute-start.4 = (bf16[8,4096]{1,0:T(8,128)(2,1)S(1)}, bf16[8,4096]{1,0:T(8,128)(2,1)S(1)}, u32[]{:S(2)}, u32[]{:S(2)}) collective-permute-start(bf16[8,4096]{1,0:T(8,128)(2,1)S(1)} %pad_maximum_fusion.1.refs_1_), channel_id=1, source_target_pairs={{0,2},{2,0},{4,6},{6,4},{8,10},{10,8},{12,14},{14,12},{16,18},{18,... | collective-permute-start | bytes 196616 | tf_op jit(solution)/shard_map/ppermute | solution.py:27
  13.2 7.1 %collective-permute-start.1 = (bf16[8,4096]{1,0:T(8,128)(2,1)S(1)}, bf16[8,4096]{1,0:T(8,128)(2,1)S(1)}, u32[]{:S(2)}, u32[]{:S(2)}) collective-permute-start(bf16[8,4096]{1,0:T(8,128)(2,1)S(1)} %pad_maximum_fusion.refs_0_), channel_id=1, source_target_pairs={{0,2},{2,0},{4,6},{6,4},{8,10},{10,8},{12,14},{14,12},{16,18},{18,... | collective-permute-start | bytes 196616 | tf_op jit(solution)/shard_map/ppermute | solution.py:27
  13.7 6.6 %collective-permute-start.8 = (bf16[8,4096]{1,0:T(8,128)(2,1)S(1)}, bf16[8,4096]{1,0:T(8,128)(2,1)S(1)}, u32[]{:S(2)}, u32[]{:S(2)}) collective-permute-start(bf16[8,4096]{1,0:T(8,128)(2,1)S(1)} %collective-permute-done.7.refs_3_), channel_id=1, source_target_pairs={{0,2},{2,0},{4,6},{6,4},{8,10},{10,8},{12,14},{14,12},{16,18},{18,... | collective-permute-start | bytes 196616 | tf_op jit(solution)/shard_map/ppermute | solution.py:27
  16.8 3.5 %collective-permute-start.6 = (bf16[8,4096]{1,0:T(8,128)(2,1)S(1)}, bf16[8,4096]{1,0:T(8,128)(2,1)S(1)}, u32[]{:S(2)}, u32[]{:S(2)}) collective-permute-start(bf16[8,4096]{1,0:T(8,128)(2,1)S(1)} %collective-permute-done.5.refs_2_), channel_id=1, source_target_pairs={{0,2},{2,0},{4,6},{6,4},{8,10},{10,8},{12,14},{14,12},{16,18},{18,... | collective-permute-start | bytes 196616 | tf_op jit(solution)/shard_map/ppermute | solution.py:27
  16.8 3.5 %copy-start.3 = (s32[256]{0:T(256)S(1)}, s32[256]{0:T(256)}, u32[]{:S(2)}) copy-start(s32[256]{0:T(256)} %param.9) | copy-start | bytes 3076
  16.8 3.5 %copy-start.4 = (f32[256]{0:T(256)S(1)}, f32[256]{0:T(256)}, u32[]{:S(2)}) copy-start(f32[256]{0:T(256)} %param.13) | copy-start | bytes 3076
  19.5 0.8 %copy-start.2 = (f32[64,256]{1,0:T(8,128)S(1)}, f32[64,256]{1,0:T(8,128)}, u32[]{:S(2)}) copy-start(f32[64,256]{1,0:T(8,128)} %get-tuple-element.22.refs_8_) | copy-start | bytes 196612
  19.5 0.8 %copy-start.5 = (f32[1,256]{1,0:T(1,128)S(1)}, f32[1,256]{1,0:T(1,128)}, u32[]{:S(2)}) copy-start(f32[1,256]{1,0:T(1,128)} %get-tuple-element.23.refs_9_) | copy-start | bytes 3076
  22.0 1.7 %collective-permute-start.9 = (bf16[32,4096]{1,0:T(8,128)(2,1)S(1)}, bf16[32,4096]{1,0:T(8,128)(2,1)S(1)}, u32[]{:S(2)}, u32[]{:S(2)}) collective-permute-start(bf16[32,4096]{1,0:T(8,128)(2,1)S(1)} %get-tuple-element.28), channel_id=1, source_target_pairs={{0,2},{2,0},{4,6},{6,4},{8,10},{10,8},{12,14},{14,12},{16,18},{18,... | collective-permute-start | bytes 786440 | tf_op jit(solution)/shard_map/ppermute | solution.py:27
  23.8 3.9 %collective-permute-start.10 = (bf16[8,4096]{1,0:T(8,128)(2,1)S(1)}, bf16[8,4096]{1,0:T(8,128)(2,1)S(1)}, u32[]{:S(2)}, u32[]{:S(2)}) collective-permute-start(bf16[8,4096]{1,0:T(8,128)(2,1)S(1)} %get-tuple-element.30), channel_id=1, source_target_pairs={{0,6},{2,4},{4,2},{6,0},{8,14},{10,12},{12,10},{14,8},{16,22},{18,... | collective-permute-start | bytes 196616 | tf_op jit(solution)/shard_map/ppermute | solution.py:27
  24.3 4.7 %collective-permute-start.12 = (bf16[8,4096]{1,0:T(8,128)(2,1)S(1)}, bf16[8,4096]{1,0:T(8,128)(2,1)S(1)}, u32[]{:S(2)}, u32[]{:S(2)}) collective-permute-start(bf16[8,4096]{1,0:T(8,128)(2,1)S(1)} %get-tuple-element.34), channel_id=1, source_target_pairs={{0,6},{2,4},{4,2},{6,0},{8,14},{10,12},{12,10},{14,8},{16,22},{18,... | collective-permute-start | bytes 196616 | tf_op jit(solution)/shard_map/ppermute | solution.py:27
  27.7 5.1 %collective-permute-start.11 = (bf16[4,4096]{1,0:T(4,128)(2,1)S(1)}, bf16[4,4096]{1,0:T(4,128)(2,1)S(1)}, u32[]{:S(2)}, u32[]{:S(2)}) collective-permute-start(bf16[4,4096]{1,0:T(4,128)(2,1)S(1)} %get-tuple-element.32), channel_id=1, source_target_pairs={{0,10},{2,8},{4,14},{6,12},{8,2},{10,0},{12,6},{14,4},{16,26},{18,... | collective-permute-start | bytes 98312 | tf_op jit(solution)/shard_map/ppermute | solution.py:27
  29.1 4.3 %collective-permute-start.13 = (bf16[4,4096]{1,0:T(4,128)(2,1)S(1)}, bf16[4,4096]{1,0:T(4,128)(2,1)S(1)}, u32[]{:S(2)}, u32[]{:S(2)}) collective-permute-start(bf16[4,4096]{1,0:T(4,128)(2,1)S(1)} %get-tuple-element.35), channel_id=1, source_target_pairs={{0,18},{2,16},{4,22},{6,20},{8,26},{10,24},{12,30},{14,28},{16,2},... | collective-permute-start | bytes 98312 | tf_op jit(solution)/shard_map/ppermute | solution.py:27
  30.3 5.2 %collective-permute-start.14 = (bf16[4,4096]{1,0:T(4,128)(2,1)S(1)}, bf16[4,4096]{1,0:T(4,128)(2,1)S(1)}, u32[]{:S(2)}, u32[]{:S(2)}) collective-permute-start(bf16[4,4096]{1,0:T(4,128)(2,1)S(1)} %get-tuple-element.36), channel_id=1, source_target_pairs={{0,26},{2,24},{4,30},{6,28},{8,18},{10,16},{12,22},{14,20},{16,10}... | collective-permute-start | bytes 98312 | tf_op jit(solution)/shard_map/ppermute | solution.py:27
  35.5 5.9 %collective-permute-start.15 = (bf16[4,4096]{1,0:T(4,128)(2,1)S(1)}, bf16[4,4096]{1,0:T(4,128)(2,1)S(1)}, u32[]{:S(2)}, u32[]{:S(2)}) collective-permute-start(bf16[4,4096]{1,0:T(4,128)(2,1)S(1)} %get-tuple-element.37), channel_id=1, source_target_pairs={{0,1},{1,0},{2,3},{3,2},{4,5},{5,4},{6,7},{7,6},{8,9},{9,8},{10,11... | collective-permute-start | bytes 98312 | tf_op jit(solution)/shard_map/ppermute | solution.py:27
  39.3 2.2 %copy-start.1 = (bf16[4,4096]{1,0:T(4,128)(2,1)S(1)}, bf16[4,4096]{1,0:T(4,128)(2,1)}, u32[]{:S(2)}) copy-start(bf16[4,4096]{1,0:T(4,128)(2,1)} %p_ref.1) | copy-start | bytes 98308

commit v2 on v1

--- a/solution.py
+++ b/solution.py
@@ -53,23 +53,17 @@
     return owner * block + (row - place * block)
 
 
-def prepare_kernel(
-    stages, block, me_ref, ids_hbm, mask_hbm, count_hbm, q_hbm, w_ref, qs_ref, q_ref, ids_ref, mask_ref, count_ref, sems
+def weight_kernel(
+    stages, block, me_ref, ids_hbm, mask_hbm, count_hbm, unused_hbm, w_ref, ids_ref, mask_ref, count_ref, sems
 ):
-    parts = sems.shape[0] - 3
-    rows = q_ref.shape[0] // parts
-    small = [
-        pltpu.make_async_copy(src, dst, sems.at[parts + k])
+    copies = [
+        pltpu.make_async_copy(src, dst, sems.at[k])
         for k, (src, dst) in enumerate(((ids_hbm, ids_ref), (mask_hbm, mask_ref), (count_hbm, count_ref)))
     ]
-    large = [
-        pltpu.make_async_copy(q_hbm.at[pl.ds(k * rows, rows)], q_ref.at[pl.ds(k * rows, rows)], sems.at[k])
-        for k in range(parts)
-    ]
-    for copy in small + large:
+    for copy in copies:
         copy.start()
     columns = passage_ids(stages, block, w_ref.shape, me_ref[0])
-    for copy in small:
+    for copy in copies:
         copy.wait()
     slots = ids_ref.shape[0]
     slot = lax.broadcasted_iota(jnp.int32, ids_ref.shape, 0)
@@ -78,13 +72,6 @@
     for k in range(slots):
         weights = weights + jnp.where(named[k : k + 1] == columns, 1.0, 0.0)
     w_ref[...] = weights
-    scales = []
-    for k in range(parts):
-        large[k].wait()
-        f = wide(q_ref[k * rows : (k + 1) * rows])
-        scales.append(lax.rsqrt(jnp.sum(f * f, axis=1, keepdims=True) + norm_eps))
-    scale = jnp.concatenate(scales, axis=0)
-    qs_ref[...] = jnp.broadcast_to(scale, (scale.shape[0], 128)).T[:1]
 
 
 def raw_and_scale(refs, q):
@@ -94,11 +81,20 @@
     return lax.dot_general(rows, q, ROWS, preferred_element_type=jnp.float32), scale
 
 
-def first_kernel(n, *refs):
-    q_ref, raw_ref, scale_ref = refs[n:]
-    raw, scale = raw_and_scale(refs[:n], q_ref[...])
+def early_kernel(n, *refs):
+    q_ref, raw_ref, scale_ref, qs_ref = refs[n:]
+    q = q_ref[...]
+    raw, scale = raw_and_scale(refs[:n], q)
     raw_ref[...] = raw
     scale_ref[...] = jnp.broadcast_to(scale, scale_ref.shape)
+    f = wide(q)
+    own = lax.rsqrt(jnp.sum(f * f, axis=1, keepdims=True) + norm_eps)
+    qs_ref[...] = jnp.broadcast_to(own, (own.shape[0], 128)).T[:1]
+
+
+def interleave(first, second):
+    part = first.shape[0] // 2
+    return jnp.concatenate([first[:part], second[:part], first[part:], second[part:]], axis=0)
 
 
 def loss_kernel(n, stages, block, *refs):
@@ -108,8 +104,8 @@
     q = q_ref[...]
     qs = qs_ref[...]
     rawb, scaleb = raw_and_scale(refs[:n], q)
-    raw = jnp.concatenate([rawa_ref[...], rawb], axis=0)
-    scale = jnp.concatenate([scalea_ref[:, :1], scaleb], axis=0)
+    raw = interleave(rawa_ref[...], rawb)
+    scale = interleave(scalea_ref[:, :1], scaleb)
     scores = logit_scale * (raw * scale * qs)
     terms = w_ref[...] * jnp.exp(scores)
     denom = jnp.sum(terms, axis=0, keepdims=True)
@@ -207,35 +203,36 @@
         half = pool_size // 2
 
         f32 = jnp.float32
-        parts = 4
-        weights, qs = pl.pallas_call(
-            functools.partial(prepare_kernel, stages, block),
-            out_shape=(
-                jax.ShapeDtypeStruct((pool_size, count), f32),
-                jax.ShapeDtypeStruct((1, count), f32),
-            ),
+        weights = pl.pallas_call(
+            functools.partial(weight_kernel, stages, block),
+            out_shape=jax.ShapeDtypeStruct((pool_size, count), f32),
             in_specs=[SMEM] + [pl.BlockSpec(memory_space=pltpu.HBM)] * 4,
-            out_specs=(VMEM,) * 2,
+            out_specs=VMEM,
             scratch_shapes=[
-                pltpu.VMEM(queries.shape, queries.dtype),
                 pltpu.VMEM(neg_ids.shape[::-1], jnp.int32),
                 pltpu.VMEM(neg_ids.shape[::-1], jnp.int32),
                 pltpu.VMEM((1, count), jnp.int32),
-                pltpu.SemaphoreType.DMA((parts + 3,)),
+                pltpu.SemaphoreType.DMA((3,)),
             ],
-            cost_estimate=cost(10000000, 3000000),
+            cost_estimate=cost(10000000, 200000),
             compiler_params=WIDE_LIMIT,
-            name="prepare",
+            name="weights",
         )(me_arr, neg_ids.T, neg_mask.T, neg_counts.reshape(1, count), queries)
-        rawa, scalea = pl.pallas_call(
-            functools.partial(first_kernel, n),
-            out_shape=(jax.ShapeDtypeStruct((half, count), f32), jax.ShapeDtypeStruct((half, 128), f32)),
+        early = pool[: n // 2] + pool[n : n + n // 2]
+        late = pool[n // 2 : n] + pool[n + n // 2 :]
+        rawa, scalea, qs = pl.pallas_call(
+            functools.partial(early_kernel, n),
+            out_shape=(
+                jax.ShapeDtypeStruct((half, count), f32),
+                jax.ShapeDtypeStruct((half, 128), f32),
+                jax.ShapeDtypeStruct((1, count), f32),
+            ),
             in_specs=[VMEM] * (n + 1),
-            out_specs=(VMEM, VMEM),
+            out_specs=(VMEM,) * 3,
             cost_estimate=cost(2 * half * count * width, 2000000),
             compiler_params=LIMIT,
-            name="first_scores",
-        )(*pool[:n], queries)
+            name="early_scores",
+        )(*early, queries)
         sent, pa, qc, loss, inner = pl.pallas_call(
             functools.partial(loss_kernel, n, stages, block),
             out_shape=(
@@ -250,7 +247,7 @@
             cost_estimate=cost(4 * half * count * width, 2000000),
             compiler_params=LIMIT,
             name="loss",
-        )(*pool[n:], me_arr, queries, rawa, scalea, weights, qs, pos_ids.reshape(1, count), d_loss.reshape(1, count))
+        )(*late, me_arr, queries, rawa, scalea, weights, qs, pos_ids.reshape(1, count), d_loss.reshape(1, count))
         total = pl.pallas_call(
             kept_kernel,
             out_shape=jax.ShapeDtypeStruct((half, width), f32),

time: 42.6 us -> 41.7 us (0.979)
  Pallas kernels: 10.7 us -> 9.83 us
    pallas_call x2, Pallas kernels: 3.38 us -> 2.45 us  [the longest x1 1.69 us: body(): pl.pallas_call(functools.partial(weight_kernel, stages, block), out_shape...]
  transfers between devices with their start and end apart: 16 -> 16, of which waited for: 9 -> 9; matrix products, arithmetic and copies ran while one was open for 2% -> 2% of each run, Pallas kernels for 19% -> 18%
where the time goes in v2:
time: 41.7 us; the launch traced here: 41.4 us
  starting transfers between devices  17.1 us (41%)
  waiting for transfers between devices  12.8 us (31%)
  Pallas kernels  9.83 us (24%)
  other arithmetic  0.87 us (2%)
  between operations  0.74 us (2%)
    ppermute x16, starting transfers between devices, swap(): return lax.ppermute(x, axis, [(i, i ^ mask) for i in range(size)])  17.1 us
    ppermute x16, waiting for transfers between devices, swap(): return lax.ppermute(x, axis, [(i, i ^ mask) for i in range(size)])  12.8 us
    pallas_call x2, Pallas kernels, body(): pl.pallas_call(functools.partial(query_kernel, 2 * n, k * steps), out_sha...  4.37 us
    pallas_call x1, Pallas kernels, body(): pl.pallas_call(functools.partial(weight_kernel, stages, block), out_shape...  1.69 us
    pallas_call x1, Pallas kernels, body(): pl.pallas_call(functools.partial(loss_kernel, n, stages, block), out_shap...  1.61 us
    pallas_call x1, Pallas kernels, body(): pl.pallas_call(functools.partial(passage_kernel, len(moved)), out_shape=j...  0.86 us
  transfers between devices with their start and end apart: 16, of which 9 were waited for; matrix products, arithmetic and copies ran while one was open for 2% of the time, Pallas kernels for 18%

profile of v2, /device:TPU:0, one launch (start us, length us, event | category | flops | bytes accessed | tf_op | source)
XLA Modules:
  0.0 41.4 jit_solution(4288608966117286156)
XLA Ops:
  0.6 0.0 copy-start
  0.6 3.6 %collective-permute-start.2 = (bf16[4,4096]{1,0:T(4,128)(2,1)}, bf16[4,4096]{1,0:T(4,128)(2,1)S(1)}, u32[]{:S(2)}, u32[]{:S(2)}) collective-permute-start(bf16[4,4096]{1,0:T(4,128)(2,1)} %p_ref.1), channel_id=1, source_target_pairs={{0,18},{2,16},{4,22},{6,20},{8,26},{10,24},{12,30},{14,28},{16,2},... | collective-permute-start | bytes 98312 | tf_op jit(solution)/shard_map/ppermute | solution.py:27
  4.2 1.6 %collective-permute-start.3 = (bf16[4,4096]{1,0:T(4,128)(2,1)}, bf16[4,4096]{1,0:T(4,128)(2,1)S(1)}, u32[]{:S(2)}, u32[]{:S(2)}) collective-permute-start(bf16[4,4096]{1,0:T(4,128)(2,1)} %p_ref.1), channel_id=1, source_target_pairs={{0,26},{2,24},{4,30},{6,28},{8,18},{10,16},{12,22},{14,20},{16,10}... | collective-permute-start | bytes 98312 | tf_op jit(solution)/shard_map/ppermute | solution.py:27
  5.8 0.2 collective-permute-start
  6.1 0.2 collective-permute-done.2
  6.3 3.4 %collective-permute-done.3 = bf16[4,4096]{1,0:T(4,128)(2,1)S(1)} collective-permute-done((bf16[4,4096]{1,0:T(4,128)(2,1)}, bf16[4,4096]{1,0:T(4,128)(2,1)S(1)}, u32[]{:S(2)}, u32[]{:S(2)}) %collective-permute-start.3) | collective-permute-done | bytes 32800 | tf_op jit(solution)/shard_map/ppermute | solution.py:27
  9.7 2.0 %collective-permute-start.4 = (bf16[8,4096]{1,0:T(8,128)(2,1)S(1)}, bf16[8,4096]{1,0:T(8,128)(2,1)S(1)}, u32[]{:S(2)}, u32[]{:S(2)}) collective-permute-start(bf16[8,4096]{1,0:T(8,128)(2,1)S(1)} %pad_maximum_fusion.1.refs_1_), channel_id=1, source_target_pairs={{0,6},{2,4},{4,2},{6,0},{8,14},{10,12},{12,10},{14,8},{16,22},{18,... | collective-permute-start | bytes 196616 | tf_op jit(solution)/shard_map/ppermute | solution.py:27
  11.7 0.0 collective-permute-done
  11.7 0.8 %pad_maximum_fusion.refs_0_ = bf16[8,4096]{1,0:T(8,128)(2,1)S(1)} fusion(bf16[4,4096]{1,0:T(4,128)(2,1)S(1)} %collective-permute-done, bf16[4,4096]{1,0:T(4,128)(2,1)} %p_ref.1), kind=kLoop, calls=%fused_computation | loop fusion | flops 131072 | bytes 131072 | tf_op jit(solution)/shard_map/concatenate | solution.py:196
  12.5 0.1 collective-permute-start.1
  12.6 0.6 %collective-permute-start.8 = (bf16[8,4096]{1,0:T(8,128)(2,1)S(1)}, bf16[8,4096]{1,0:T(8,128)(2,1)S(1)}, u32[]{:S(2)}, u32[]{:S(2)}) collective-permute-start(bf16[8,4096]{1,0:T(8,128)(2,1)S(1)} %pad_maximum_fusion.1.refs_1_), channel_id=1, source_target_pairs={{0,2},{2,0},{4,6},{6,4},{8,10},{10,8},{12,14},{14,12},{16,18},{18,... | collective-permute-start | bytes 196616 | tf_op jit(solution)/shard_map/ppermute | solution.py:27
  13.2 0.0 collective-permute-start.7
  13.2 0.5 %collective-permute-done.4.refs_1_.refs_3_ = bf16[8,4096]{1,0:T(8,128)(2,1)S(1)} collective-permute-done((bf16[8,4096]{1,0:T(8,128)(2,1)S(1)}, bf16[8,4096]{1,0:T(8,128)(2,1)S(1)}, u32[]{:S(2)}, u32[]{:S(2)}) %collective-permute-start.4) | collective-permute-done | bytes 65568 | tf_op jit(solution)/shard_map/ppermute | solution.py:27
  13.7 0.6 %collective-permute-start.6 = (bf16[8,4096]{1,0:T(8,128)(2,1)S(1)}, bf16[8,4096]{1,0:T(8,128)(2,1)S(1)}, u32[]{:S(2)}, u32[]{:S(2)}) collective-permute-start(bf16[8,4096]{1,0:T(8,128)(2,1)S(1)} %collective-permute-done.4.refs_1_.refs_3_), channel_id=1, source_target_pairs={{0,2},{2,0},{4,6},{6,4},{8,10},{10,8},{12,14},{14,12},{16,18},{18,... | collective-permute-start | bytes 196616 | tf_op jit(solution)/shard_map/ppermute | solution.py:27
  14.3 2.6 %collective-permute-done.1.refs_0_.refs_2_ = bf16[8,4096]{1,0:T(8,128)(2,1)S(1)} collective-permute-done((bf16[8,4096]{1,0:T(8,128)(2,1)S(1)}, bf16[8,4096]{1,0:T(8,128)(2,1)S(1)}, u32[]{:S(2)}, u32[]{:S(2)}) %collective-permute-start.1) | collective-permute-done | bytes 65568 | tf_op jit(solution)/shard_map/ppermute | solution.py:27
  16.8 0.0 collective-permute-start.5
  16.8 0.0 copy-start.3
  16.8 1.7 %weights.1.refs_8_ = f32[64,256]{1,0:T(8,128)} custom-call(s32[1]{0:T(128)} %bitcast.me_ref.refs_4_, s32[32,256]{1,0:T(8,128)} %bitcast.9, s32[32,256]{1,0:T(8,128)} %bitcast.10, s32[1,256]{1,0:T(1,128)} %bitcast.11, bf16[256,4096]{1,0:T(8,128)(2,1)} %q_ref.1), custom_call_target="tpu_custom_call" | custom-call | flops 10000000 | bytes 200000 | tf_op jit(solution)/shard_map/weights/pallas_call | solution.py:206
  18.5 0.0 copy-start.1
  18.6 0.0 collective-permute-done.8.refs_3_.refs_5_
  18.6 0.0 collective-permute-done.7.refs_2_.refs_4_
  18.6 0.0 copy-done
  18.6 0.8 %early_scores.1 = (f32[32,256]{1,0:T(8,128)S(1)}, f32[32,128]{1,0:T(8,128)S(1)}, f32[1,256]{1,0:T(1,128)S(1)}) custom-call(bf16[8,4096]{1,0:T(8,128)(2,1)S(1)} %pad_maximum_fusion.refs_0_, bf16[8,4096]{1,0:T(8,128)(2,1)S(1)} %pad_maximum_fusion.1.refs_1_, bf16[8,4096]{1,0:T(8,128)(2,1)S(1)} %collective-permute-done.7.refs_2_.refs_4_, ...), custom_call_target="tpu_custom_call" | custom-call | flops 67108864 | bytes 2000000 | tf_op jit(solution)/shard_map/early_scores/pallas_call | solution.py:223
  19.3 0.0 collective-permute-done.6.refs_3_.refs_7_
  19.4 0.0 collective-permute-done.5.refs_2_.refs_6_
  19.4 0.0 copy-done.3
  19.4 0.0 copy-done.4
  19.4 0.0 copy-done.1
  19.4 1.6 %loss.1 = (bf16[32,4096]{1,0:T(8,128)(2,1)S(1)}, bf16[32,256]{1,0:T(8,128)(2,1)S(1)}, bf16[64,256]{1,0:T(8,128)(2,1)S(1)}, f32[1,256]{1,0:T(1,128)}, f32[1,256]{1,0:T(1,128)S(1)}) custom-call(bf16[8,4096]{1,0:T(8,128)(2,1)S(1)} %collective-permute-done.1.refs_0_.refs_2_, bf16[8,4096]{1,0:T(8,128)(2,1)S(1)} %collective-permute-done.4.refs_1_.refs_3_, ...), custom_call_target="tpu_custom_call" | custom-call | flops 134217728 | bytes 2000000 | tf_op jit(solution)/shard_map/loss/pallas_call | solution.py:236
  21.0 0.6 %collective-permute-start.9 = (bf16[32,4096]{1,0:T(8,128)(2,1)S(1)}, bf16[32,4096]{1,0:T(8,128)(2,1)S(1)}, u32[]{:S(2)}, u32[]{:S(2)}) collective-permute-start(bf16[32,4096]{1,0:T(8,128)(2,1)S(1)} %get-tuple-element.26), channel_id=1, source_target_pairs={{0,2},{2,0},{4,6},{6,4},{8,10},{10,8},{12,14},{14,12},{16,18},{18,... | collective-permute-start | bytes 786440 | tf_op jit(solution)/shard_map/ppermute | solution.py:27
  21.6 0.5 %kept_terms.1.total_ref = f32[32,4096]{1,0:T(8,128)S(1)} custom-call(bf16[32,256]{1,0:T(8,128)(2,1)S(1)} %get-tuple-element.25.pa_ref, bf16[256,4096]{1,0:T(8,128)(2,1)S(1)} %copy-done), custom_call_target="tpu_custom_call" | custom-call | flops 67108864 | bytes 2000000 | tf_op jit(solution)/shard_map/kept_terms/pallas_call | solution.py:251
  22.0 0.7 %collective-permute-done.9.got_ref = bf16[32,4096]{1,0:T(8,128)(2,1)S(1)} collective-permute-done((bf16[32,4096]{1,0:T(8,128)(2,1)S(1)}, bf16[32,4096]{1,0:T(8,128)(2,1)S(1)}, u32[]{:S(2)}, u32[]{:S(2)}) %collective-permute-start.9) | collective-permute-done | bytes 262176 | tf_op jit(solution)/shard_map/ppermute | solution.py:27
  22.8 0.6 %collective-permute-start.10 = (bf16[8,4096]{1,0:T(8,128)(2,1)S(1)}, bf16[8,4096]{1,0:T(8,128)(2,1)S(1)}, u32[]{:S(2)}, u32[]{:S(2)}) collective-permute-start(bf16[8,4096]{1,0:T(8,128)(2,1)S(1)} %get-tuple-element.28), channel_id=1, source_target_pairs={{0,6},{2,4},{4,2},{6,0},{8,14},{10,12},{12,10},{14,8},{16,22},{18,... | collective-permute-start | bytes 196616 | tf_op jit(solution)/shard_map/ppermute | solution.py:27
  23.4 1.2 %collective-permute-start.12 = (bf16[8,4096]{1,0:T(8,128)(2,1)S(1)}, bf16[8,4096]{1,0:T(8,128)(2,1)S(1)}, u32[]{:S(2)}, u32[]{:S(2)}) collective-permute-start(bf16[8,4096]{1,0:T(8,128)(2,1)S(1)} %get-tuple-element.32), channel_id=1, source_target_pairs={{0,6},{2,4},{4,2},{6,0},{8,14},{10,12},{12,10},{14,8},{16,22},{18,... | collective-permute-start | bytes 196616 | tf_op jit(solution)/shard_map/ppermute | solution.py:27
  24.6 2.1 %collective-permute-done.10.got_ref = bf16[8,4096]{1,0:T(8,128)(2,1)S(1)} collective-permute-done((bf16[8,4096]{1,0:T(8,128)(2,1)S(1)}, bf16[8,4096]{1,0:T(8,128)(2,1)S(1)}, u32[]{:S(2)}, u32[]{:S(2)}) %collective-permute-start.10) | collective-permute-done | bytes 65568 | tf_op jit(solution)/shard_map/ppermute | solution.py:27
  26.7 0.7 %collective-permute-start.11 = (bf16[4,4096]{1,0:T(4,128)(2,1)S(1)}, bf16[4,4096]{1,0:T(4,128)(2,1)S(1)}, u32[]{:S(2)}, u32[]{:S(2)}) collective-permute-start(bf16[4,4096]{1,0:T(4,128)(2,1)S(1)} %get-tuple-element.30), channel_id=1, source_target_pairs={{0,10},{2,8},{4,14},{6,12},{8,2},{10,0},{12,6},{14,4},{16,26},{18,... | collective-permute-start | bytes 98312 | tf_op jit(solution)/shard_map/ppermute | solution.py:27
  27.4 0.7 %collective-permute-done.12.got_ref = bf16[8,4096]{1,0:T(8,128)(2,1)S(1)} collective-permute-done((bf16[8,4096]{1,0:T(8,128)(2,1)S(1)}, bf16[8,4096]{1,0:T(8,128)(2,1)S(1)}, u32[]{:S(2)}, u32[]{:S(2)}) %collective-permute-start.12) | collective-permute-done | bytes 65568 | tf_op jit(solution)/shard_map/ppermute | solution.py:27
  28.1 1.2 %collective-permute-start.13 = (bf16[4,4096]{1,0:T(4,128)(2,1)S(1)}, bf16[4,4096]{1,0:T(4,128)(2,1)S(1)}, u32[]{:S(2)}, u32[]{:S(2)}) collective-permute-start(bf16[4,4096]{1,0:T(4,128)(2,1)S(1)} %get-tuple-element.33), channel_id=1, source_target_pairs={{0,18},{2,16},{4,22},{6,20},{8,26},{10,24},{12,30},{14,28},{16,2},... | collective-permute-start | bytes 98312 | tf_op jit(solution)/shard_map/ppermute | solution.py:27
  29.3 2.5 %collective-permute-start.14 = (bf16[4,4096]{1,0:T(4,128)(2,1)S(1)}, bf16[4,4096]{1,0:T(4,128)(2,1)S(1)}, u32[]{:S(2)}, u32[]{:S(2)}) collective-permute-start(bf16[4,4096]{1,0:T(4,128)(2,1)S(1)} %get-tuple-element.34), channel_id=1, source_target_pairs={{0,26},{2,24},{4,30},{6,28},{8,18},{10,16},{12,22},{14,20},{16,10}... | collective-permute-start | bytes 98312 | tf_op jit(solution)/shard_map/ppermute | solution.py:27
  31.8 0.0 collective-permute-done.11
  31.8 0.6 %collective-permute-done.13 = bf16[4,4096]{1,0:T(4,128)(2,1)S(1)} collective-permute-done((bf16[4,4096]{1,0:T(4,128)(2,1)S(1)}, bf16[4,4096]{1,0:T(4,128)(2,1)S(1)}, u32[]{:S(2)}, u32[]{:S(2)}) %collective-permute-start.13) | collective-permute-done | bytes 32800 | tf_op jit(solution)/shard_map/ppermute | solution.py:27
  32.4 2.1 %collective-permute-done.14 = bf16[4,4096]{1,0:T(4,128)(2,1)S(1)} collective-permute-done((bf16[4,4096]{1,0:T(4,128)(2,1)S(1)}, bf16[4,4096]{1,0:T(4,128)(2,1)S(1)}, u32[]{:S(2)}, u32[]{:S(2)}) %collective-permute-start.14) | collective-permute-done | bytes 32800 | tf_op jit(solution)/shard_map/ppermute | solution.py:27
  34.6 1.6 %collective-permute-start.15 = (bf16[4,4096]{1,0:T(4,128)(2,1)S(1)}, bf16[4,4096]{1,0:T(4,128)(2,1)S(1)}, u32[]{:S(2)}, u32[]{:S(2)}) collective-permute-start(bf16[4,4096]{1,0:T(4,128)(2,1)S(1)} %get-tuple-element.35), channel_id=1, source_target_pairs={{0,1},{1,0},{2,3},{3,2},{4,5},{5,4},{6,7},{7,6},{8,9},{9,8},{10,11... | collective-permute-start | bytes 98312 | tf_op jit(solution)/shard_map/ppermute | solution.py:27
  36.1 2.2 %shard_map.94.refs_11_ = bf16[256,4096]{1,0:T(8,128)(2,1)} custom-call(bf16[8,4096]{1,0:T(8,128)(2,1)S(1)} %pad_maximum_fusion.refs_0_, bf16[8,4096]{1,0:T(8,128)(2,1)S(1)} %pad_maximum_fusion.1.refs_1_, bf16[8,4096]{1,0:T(8,128)(2,1)S(1)} %collective-permute-done.1.refs_0_.refs_2_, bf16[8,4096]{1,0:T(8,128)(2,1)S(1)} %collective-permute-done.4.refs_1_.refs_3_, ...), custom_call_target="tpu_custom_call" | custom-call | flops 67108864 | bytes 2500000 | tf_op jit(solution)/shard_map/pallas_call | solution.py:292
  38.3 2.2 %shard_map.95 = bf16[256,4096]{1,0:T(8,128)(2,1)} custom-call(bf16[8,4096]{1,0:T(8,128)(2,1)S(1)} %pad_maximum_fusion.refs_0_, bf16[8,4096]{1,0:T(8,128)(2,1)S(1)} %pad_maximum_fusion.1.refs_1_, bf16[8,4096]{1,0:T(8,128)(2,1)S(1)} %collective-permute-done.1.refs_0_.refs_2_, ...), custom_call_target="tpu_custom_call", output_to_operand_aliasing={{}: (11, {})} | custom-call | flops 67108864 | bytes 2500000 | tf_op jit(solution)/shard_map/pallas_call | solution.py:292
  40.5 0.0 collective-permute-done.15.refs_0_
  40.5 0.0 copy-done.2
  40.5 0.9 %passage_gradients.1 = bf16[4,4096]{1,0:T(4,128)(2,1)} custom-call(bf16[4,4096]{1,0:T(4,128)(2,1)S(1)} %copy-done.2, f32[4,4096]{1,0:T(4,128)S(1)} %get-tuple-element.36.total_ref, bf16[4,4096]{1,0:T(4,128)(2,1)S(1)} %collective-permute-done.15.refs_0_), custom_call_target="tpu_custom_call" | custom-call | flops 1000000 | bytes 200000 | tf_op jit(solution)/shard_map/passage_gradients/pallas_call | solution.py:303
  (7 shorter events, 0.2 us)
Async XLA Ops:
  0.6 17.9 %copy-start = (bf16[256,4096]{1,0:T(8,128)(2,1)S(1)}, bf16[256,4096]{1,0:T(8,128)(2,1)}, u32[]{:S(2)}) copy-start(bf16[256,4096]{1,0:T(8,128)(2,1)} %q_ref.1) | copy-start | bytes 6291460
  0.6 5.7 %collective-permute-start.2 = (bf16[4,4096]{1,0:T(4,128)(2,1)}, bf16[4,4096]{1,0:T(4,128)(2,1)S(1)}, u32[]{:S(2)}, u32[]{:S(2)}) collective-permute-start(bf16[4,4096]{1,0:T(4,128)(2,1)} %p_ref.1), channel_id=1, source_target_pairs={{0,18},{2,16},{4,22},{6,20},{8,26},{10,24},{12,30},{14,28},{16,2},... | collective-permute-start | bytes 98312 | tf_op jit(solution)/shard_map/ppermute | solution.py:27
  4.2 5.4 %collective-permute-start.3 = (bf16[4,4096]{1,0:T(4,128)(2,1)}, bf16[4,4096]{1,0:T(4,128)(2,1)S(1)}, u32[]{:S(2)}, u32[]{:S(2)}) collective-permute-start(bf16[4,4096]{1,0:T(4,128)(2,1)} %p_ref.1), channel_id=1, source_target_pairs={{0,26},{2,24},{4,30},{6,28},{8,18},{10,16},{12,22},{14,20},{16,10}... | collective-permute-start | bytes 98312 | tf_op jit(solution)/shard_map/ppermute | solution.py:27
  5.8 5.9 %collective-permute-start = (bf16[4,4096]{1,0:T(4,128)(2,1)}, bf16[4,4096]{1,0:T(4,128)(2,1)S(1)}, u32[]{:S(2)}, u32[]{:S(2)}) collective-permute-start(bf16[4,4096]{1,0:T(4,128)(2,1)} %p_ref.1), channel_id=1, source_target_pairs={{0,10},{2,8},{4,14},{6,12},{8,2},{10,0},{12,6},{14,4},{16,26},{18,... | collective-permute-start | bytes 98312 | tf_op jit(solution)/shard_map/ppermute | solution.py:27
  9.7 4.0 %collective-permute-start.4 = (bf16[8,4096]{1,0:T(8,128)(2,1)S(1)}, bf16[8,4096]{1,0:T(8,128)(2,1)S(1)}, u32[]{:S(2)}, u32[]{:S(2)}) collective-permute-start(bf16[8,4096]{1,0:T(8,128)(2,1)S(1)} %pad_maximum_fusion.1.refs_1_), channel_id=1, source_target_pairs={{0,6},{2,4},{4,2},{6,0},{8,14},{10,12},{12,10},{14,8},{16,22},{18,... | collective-permute-start | bytes 196616 | tf_op jit(solution)/shard_map/ppermute | solution.py:27
  12.5 4.3 %collective-permute-start.1 = (bf16[8,4096]{1,0:T(8,128)(2,1)S(1)}, bf16[8,4096]{1,0:T(8,128)(2,1)S(1)}, u32[]{:S(2)}, u32[]{:S(2)}) collective-permute-start(bf16[8,4096]{1,0:T(8,128)(2,1)S(1)} %pad_maximum_fusion.refs_0_), channel_id=1, source_target_pairs={{0,6},{2,4},{4,2},{6,0},{8,14},{10,12},{12,10},{14,8},{16,22},{18,... | collective-permute-start | bytes 196616 | tf_op jit(solution)/shard_map/ppermute | solution.py:27
  12.6 6.0 %collective-permute-start.8 = (bf16[8,4096]{1,0:T(8,128)(2,1)S(1)}, bf16[8,4096]{1,0:T(8,128)(2,1)S(1)}, u32[]{:S(2)}, u32[]{:S(2)}) collective-permute-start(bf16[8,4096]{1,0:T(8,128)(2,1)S(1)} %pad_maximum_fusion.1.refs_1_), channel_id=1, source_target_pairs={{0,2},{2,0},{4,6},{6,4},{8,10},{10,8},{12,14},{14,12},{16,18},{18,... | collective-permute-start | bytes 196616 | tf_op jit(solution)/shard_map/ppermute | solution.py:27
  13.2 5.4 %collective-permute-start.7 = (bf16[8,4096]{1,0:T(8,128)(2,1)S(1)}, bf16[8,4096]{1,0:T(8,128)(2,1)S(1)}, u32[]{:S(2)}, u32[]{:S(2)}) collective-permute-start(bf16[8,4096]{1,0:T(8,128)(2,1)S(1)} %pad_maximum_fusion.refs_0_), channel_id=1, source_target_pairs={{0,2},{2,0},{4,6},{6,4},{8,10},{10,8},{12,14},{14,12},{16,18},{18,... | collective-permute-start | bytes 196616 | tf_op jit(solution)/shard_map/ppermute | solution.py:27
  13.7 5.7 %collective-permute-start.6 = (bf16[8,4096]{1,0:T(8,128)(2,1)S(1)}, bf16[8,4096]{1,0:T(8,128)(2,1)S(1)}, u32[]{:S(2)}, u32[]{:S(2)}) collective-permute-start(bf16[8,4096]{1,0:T(8,128)(2,1)S(1)} %collective-permute-done.4.refs_1_.refs_3_), channel_id=1, source_target_pairs={{0,2},{2,0},{4,6},{6,4},{8,10},{10,8},{12,14},{14,12},{16,18},{18,... | collective-permute-start | bytes 196616 | tf_op jit(solution)/shard_map/ppermute | solution.py:27
  16.8 2.5 %collective-permute-start.5 = (bf16[8,4096]{1,0:T(8,128)(2,1)S(1)}, bf16[8,4096]{1,0:T(8,128)(2,1)S(1)}, u32[]{:S(2)}, u32[]{:S(2)}) collective-permute-start(bf16[8,4096]{1,0:T(8,128)(2,1)S(1)} %collective-permute-done.1.refs_0_.refs_2_), channel_id=1, source_target_pairs={{0,2},{2,0},{4,6},{6,4},{8,10},{10,8},{12,14},{14,12},{16,18},{18,... | collective-permute-start | bytes 196616 | tf_op jit(solution)/shard_map/ppermute | solution.py:27
  16.8 2.5 %copy-start.3 = (s32[256]{0:T(256)S(1)}, s32[256]{0:T(256)}, u32[]{:S(2)}) copy-start(s32[256]{0:T(256)} %param.9) | copy-start | bytes 3076
  16.8 2.5 %copy-start.4 = (f32[256]{0:T(256)S(1)}, f32[256]{0:T(256)}, u32[]{:S(2)}) copy-start(f32[256]{0:T(256)} %param.13) | copy-start | bytes 3076
  18.5 0.8 %copy-start.1 = (f32[64,256]{1,0:T(8,128)S(1)}, f32[64,256]{1,0:T(8,128)}, u32[]{:S(2)}) copy-start(f32[64,256]{1,0:T(8,128)} %weights.1.refs_8_) | copy-start | bytes 196612
  21.0 1.7 %collective-permute-start.9 = (bf16[32,4096]{1,0:T(8,128)(2,1)S(1)}, bf16[32,4096]{1,0:T(8,128)(2,1)S(1)}, u32[]{:S(2)}, u32[]{:S(2)}) collective-permute-start(bf16[32,4096]{1,0:T(8,128)(2,1)S(1)} %get-tuple-element.26), channel_id=1, source_target_pairs={{0,2},{2,0},{4,6},{6,4},{8,10},{10,8},{12,14},{14,12},{16,18},{18,... | collective-permute-start | bytes 786440 | tf_op jit(solution)/shard_map/ppermute | solution.py:27
  22.8 3.9 %collective-permute-start.10 = (bf16[8,4096]{1,0:T(8,128)(2,1)S(1)}, bf16[8,4096]{1,0:T(8,128)(2,1)S(1)}, u32[]{:S(2)}, u32[]{:S(2)}) collective-permute-start(bf16[8,4096]{1,0:T(8,128)(2,1)S(1)} %get-tuple-element.28), channel_id=1, source_target_pairs={{0,6},{2,4},{4,2},{6,0},{8,14},{10,12},{12,10},{14,8},{16,22},{18,... | collective-permute-start | bytes 196616 | tf_op jit(solution)/shard_map/ppermute | solution.py:27
  23.4 4.7 %collective-permute-start.12 = (bf16[8,4096]{1,0:T(8,128)(2,1)S(1)}, bf16[8,4096]{1,0:T(8,128)(2,1)S(1)}, u32[]{:S(2)}, u32[]{:S(2)}) collective-permute-start(bf16[8,4096]{1,0:T(8,128)(2,1)S(1)} %get-tuple-element.32), channel_id=1, source_target_pairs={{0,6},{2,4},{4,2},{6,0},{8,14},{10,12},{12,10},{14,8},{16,22},{18,... | collective-permute-start | bytes 196616 | tf_op jit(solution)/shard_map/ppermute | solution.py:27
  26.7 5.1 %collective-permute-start.11 = (bf16[4,4096]{1,0:T(4,128)(2,1)S(1)}, bf16[4,4096]{1,0:T(4,128)(2,1)S(1)}, u32[]{:S(2)}, u32[]{:S(2)}) collective-permute-start(bf16[4,4096]{1,0:T(4,128)(2,1)S(1)} %get-tuple-element.30), channel_id=1, source_target_pairs={{0,10},{2,8},{4,14},{6,12},{8,2},{10,0},{12,6},{14,4},{16,26},{18,... | collective-permute-start | bytes 98312 | tf_op jit(solution)/shard_map/ppermute | solution.py:27
  28.1 4.3 %collective-permute-start.13 = (bf16[4,4096]{1,0:T(4,128)(2,1)S(1)}, bf16[4,4096]{1,0:T(4,128)(2,1)S(1)}, u32[]{:S(2)}, u32[]{:S(2)}) collective-permute-start(bf16[4,4096]{1,0:T(4,128)(2,1)S(1)} %get-tuple-element.33), channel_id=1, source_target_pairs={{0,18},{2,16},{4,22},{6,20},{8,26},{10,24},{12,30},{14,28},{16,2},... | collective-permute-start | bytes 98312 | tf_op jit(solution)/shard_map/ppermute | solution.py:27
  29.3 5.2 %collective-permute-start.14 = (bf16[4,4096]{1,0:T(4,128)(2,1)S(1)}, bf16[4,4096]{1,0:T(4,128)(2,1)S(1)}, u32[]{:S(2)}, u32[]{:S(2)}) collective-permute-start(bf16[4,4096]{1,0:T(4,128)(2,1)S(1)} %get-tuple-element.34), channel_id=1, source_target_pairs={{0,26},{2,24},{4,30},{6,28},{8,18},{10,16},{12,22},{14,20},{16,10}... | collective-permute-start | bytes 98312 | tf_op jit(solution)/shard_map/ppermute | solution.py:27
  34.6 5.9 %collective-permute-start.15 = (bf16[4,4096]{1,0:T(4,128)(2,1)S(1)}, bf16[4,4096]{1,0:T(4,128)(2,1)S(1)}, u32[]{:S(2)}, u32[]{:S(2)}) collective-permute-start(bf16[4,4096]{1,0:T(4,128)(2,1)S(1)} %get-tuple-element.35), channel_id=1, source_target_pairs={{0,1},{1,0},{2,3},{3,2},{4,5},{5,4},{6,7},{7,6},{8,9},{9,8},{10,11... | collective-permute-start | bytes 98312 | tf_op jit(solution)/shard_map/ppermute | solution.py:27
  38.3 2.2 %copy-start.2 = (bf16[4,4096]{1,0:T(4,128)(2,1)S(1)}, bf16[4,4096]{1,0:T(4,128)(2,1)}, u32[]{:S(2)}) copy-start(bf16[4,4096]{1,0:T(4,128)(2,1)} %p_ref.1) | copy-start | bytes 98308
